TPU v7x, 32 devices: a whole 2x2x4 slice. The times are simulated.
32 devices in a mesh: row: 16 (over z, y, core), col: 2 (over x).
Axes of the slice: x: 2, y: 2, z: 4, core: 2. Of those that a mesh axis runs over, the one named last changes fastest.
Arguments:
- node_features: float32 [4096, 128], P(('row', 'col')), may hold values from -6 to 6
- block_values: float32 [16, 2, 4, 128, 128], P('row', 'col')
- block_rows: int32 [16, 2, 4], P('row', 'col'), may hold values from 0 to 1, as said below
- block_cols: int32 [16, 2, 4], P('row', 'col'), may hold values from 0 to 15
- block_count: int32 [16, 2], P('row', 'col'), may hold values from 1 to 4, as said below
- w_input: float32 [128, 512], replicated, may hold values from -0.5 to 0.5
- bias_input: float32 [512], replicated, may hold values from -3 to 3
- gain_attn: float32 [512], replicated, may hold values from 0.1 to 1.9
- shift_attn: float32 [512], replicated, may hold values from -3 to 3
- w_heads: float32 [512, 1536], replicated, may hold values from -0.25 to 0.25
- w_merge: float32 [512, 512], replicated, may hold values from -0.75 to 0.75
- bias_merge: float32 [512], replicated, may hold values from -3 to 3
- gain_ffn: float32 [512], replicated, may hold values from 0.1 to 1.9
- shift_ffn: float32 [512], replicated, may hold values from -3 to 3
- w_expand: float32 [512, 1024], replicated, may hold values from -0.25 to 0.25
- bias_expand: float32 [1024], replicated, may hold values from -3 to 3
- w_reduce: float32 [1024, 512], replicated, may hold values from -0.25 to 0.25
- bias_reduce: float32 [512], replicated, may hold values from -3 to 3
- readout: float32 [512], replicated, may hold values from -0.25 to 0.25
- cotangent: float32 [4096, 512], P(('row', 'col')), may hold values from -6 to 6
Outputs:
- layer_out: float32 [4096, 512], P(('row', 'col'))
- grad_features: float32 [4096, 128], P(('row', 'col'))
- grad_w_input: float32 [128, 512], replicated
- grad_bias_input: float32 [512], replicated
- grad_gain_attn: float32 [512], replicated
- grad_shift_attn: float32 [512], replicated
- grad_w_heads: float32 [512, 1536], replicated
- grad_w_merge: float32 [512, 512], replicated
- grad_bias_merge: float32 [512], replicated
- grad_gain_ffn: float32 [512], replicated
- grad_shift_ffn: float32 [512], replicated
- grad_w_expand: float32 [512, 1024], replicated
- grad_bias_expand: float32 [1024], replicated
- grad_w_reduce: float32 [1024, 512], replicated
- grad_bias_reduce: float32 [512], replicated
- grad_readout: float32 [512], replicated
Inputs may be any that keep to these rules, and one draw needn't show every extreme that they name: Within one tile the listed (block_rows, block_cols) pairs are all different. Slots 0 to block_count - 1 of a tile are live, the rest are ignored; some tile has all 4 slots live.
All inputs are finite; a program needn't handle non-finite values.
Results may differ from a plain program's by a relative error of at most 0.0003.
Values sent between devices are 32-bit elements; how exact they have to be, the bound alone decides.
No kernel may reach another device: no remote copies, remote signals or barrier semaphores. Data moves between devices by JAX's collectives and lax.ppermute only.
A program may use at most 192 MiB of HBM per device.

v0:
```python
import math

import jax
import jax.numpy as jnp
from jax import lax
from jax.sharding import PartitionSpec as P

HEADS = 8
HEAD_DIM = 64
HOPS = 7


exact = lax.Precision.HIGHEST


def layer_norm(values, gain, shift):
    average = jnp.mean(values, axis=-1, keepdims=True)
    centred = values - average
    spread = jnp.mean(centred * centred, axis=-1, keepdims=True)
    return centred * lax.rsqrt(spread + 1e-05) * gain + shift


def node_tail(
    start,
    gain_attn,
    shift_attn,
    w_heads,
    w_merge,
    bias_merge,
    gain_ffn,
    shift_ffn,
    w_expand,
    bias_expand,
    w_reduce,
    bias_reduce,
    readout,
):
    node_count, token_count, columns = start.shape
    normed = layer_norm(start, gain_attn, shift_attn)
    projected = jnp.einsum("ntd,de->nte", normed, w_heads, precision=exact)
    queries = projected[..., :columns].reshape(node_count, token_count, HEADS, HEAD_DIM)
    key_rows = projected[..., columns : 2 * columns].reshape(
        node_count, token_count, HEADS, HEAD_DIM
    )
    value_rows = projected[..., 2 * columns :].reshape(node_count, token_count, HEADS, HEAD_DIM)
    scores = jnp.einsum("nqhe,nkhe->nhqk", queries, key_rows, precision=exact) / math.sqrt(HEAD_DIM)
    attention = jax.nn.softmax(scores, axis=-1)
    mixed = jnp.einsum("nhqk,nkhe->nqhe", attention, value_rows, precision=exact).reshape(
        node_count, token_count, columns
    )
    middle = start + jnp.einsum("ntd,de->nte", mixed, w_merge, precision=exact) + bias_merge
    normed_two = layer_norm(middle, gain_ffn, shift_ffn)
    activated = jax.nn.gelu(
        jnp.einsum("ntd,de->nte", normed_two, w_expand, precision=exact) + bias_expand,
        approximate=False,
    )
    final = middle + jnp.einsum("nte,ed->ntd", activated, w_reduce, precision=exact) + bias_reduce
    center = final[:, 0]
    others = final[:, 1:]
    weights = jax.nn.softmax(jnp.einsum("nkd,d->nk", others, readout, precision=exact), axis=-1)
    return center + jnp.einsum("nk,nkd->nd", weights, others, precision=exact)


def per_device(
    node_features,
    block_values,
    block_rows,
    block_cols,
    block_count,
    w_input,
    bias_input,
    gain_attn,
    shift_attn,
    w_heads,
    w_merge,
    bias_merge,
    gain_ffn,
    shift_ffn,
    w_expand,
    bias_expand,
    w_reduce,
    bias_reduce,
    readout,
    cotangent,
):
    values = block_values[0, 0]
    row_ids = block_rows[0, 0]
    col_ids = block_cols[0, 0]
    block_size = values.shape[-1]
    node_count = node_features.shape[0]
    row_blocks = lax.axis_size("col") * node_count // block_size
    col_blocks = lax.axis_size("row") * node_count // block_size
    is_live = (jnp.arange(values.shape[0]) < block_count[0, 0]).astype(jnp.float32)
    row_table = (row_ids[:, None] == jnp.arange(row_blocks)[None, :]).astype(jnp.float32) * is_live[
        :, None
    ]
    col_table = (col_ids[:, None] == jnp.arange(col_blocks)[None, :]).astype(jnp.float32) * is_live[
        :, None
    ]
    hop_list = [node_features]
    for hop_index in range(HOPS):
        field = hop_list[-1]
        forward_columns = field.shape[1]
        forward_gathered = lax.all_gather(field, "row", axis=0, tiled=True).reshape(
            col_blocks, block_size, forward_columns
        )
        forward_picked = forward_gathered[col_ids]
        forward_products = jnp.einsum("bij,bjw->biw", values, forward_picked, precision=exact)
        forward_partial_value = jnp.einsum(
            "br,biw->riw", row_table, forward_products, precision=exact
        ).reshape(row_blocks * block_size, forward_columns)
        hop_list.append(
            lax.psum_scatter(forward_partial_value, "col", scatter_dimension=0, tiled=True)
        )
    stacked = jnp.stack(hop_list, axis=1)

    def local_layer(
        stacked_hops,
        w_input,
        bias_input,
        gain_attn,
        shift_attn,
        w_heads,
        w_merge,
        bias_merge,
        gain_ffn,
        shift_ffn,
        w_expand,
        bias_expand,
        w_reduce,
        bias_reduce,
        readout,
    ):
        start = jnp.einsum("ntf,fd->ntd", stacked_hops, w_input, precision=exact) + bias_input
        return node_tail(
            start,
            gain_attn,
            shift_attn,
            w_heads,
            w_merge,
            bias_merge,
            gain_ffn,
            shift_ffn,
            w_expand,
            bias_expand,
            w_reduce,
            bias_reduce,
            readout,
        )

    layer_out, pullback = jax.vjp(
        local_layer,
        stacked,
        w_input,
        bias_input,
        gain_attn,
        shift_attn,
        w_heads,
        w_merge,
        bias_merge,
        gain_ffn,
        shift_ffn,
        w_expand,
        bias_expand,
        w_reduce,
        bias_reduce,
        readout,
    )
    (
        grad_hops,
        grad_w_input,
        grad_bias_input,
        grad_gain_attn,
        grad_shift_attn,
        grad_w_heads,
        grad_w_merge,
        grad_bias_merge,
        grad_gain_ffn,
        grad_shift_ffn,
        grad_w_expand,
        grad_bias_expand,
        grad_w_reduce,
        grad_bias_reduce,
        grad_readout,
    ) = pullback(cotangent)
    carried = grad_hops[:, HOPS]
    for hop_index in range(HOPS - 1, -1, -1):
        columns = carried.shape[1]
        gathered = lax.all_gather(carried, "col", axis=0, tiled=True).reshape(
            row_blocks, block_size, columns
        )
        picked = gathered[row_ids]
        products = jnp.einsum("bji,bjw->biw", values, picked, precision=exact)
        partial_value = jnp.einsum("bc,biw->ciw", col_table, products, precision=exact).reshape(
            col_blocks * block_size, columns
        )
        carried = grad_hops[:, hop_index] + lax.psum_scatter(
            partial_value, "row", scatter_dimension=0, tiled=True
        )
    summed = lax.psum(
        (
            grad_w_input,
            grad_bias_input,
            grad_gain_attn,
            grad_shift_attn,
            grad_w_heads,
            grad_w_merge,
            grad_bias_merge,
            grad_gain_ffn,
            grad_shift_ffn,
            grad_w_expand,
            grad_bias_expand,
            grad_w_reduce,
            grad_bias_reduce,
            grad_readout,
        ),
        ("row", "col"),
    )
    return (
        layer_out,
        carried,
        summed[0],
        summed[1],
        summed[2],
        summed[3],
        summed[4],
        summed[5],
        summed[6],
        summed[7],
        summed[8],
        summed[9],
        summed[10],
        summed[11],
        summed[12],
        summed[13],
    )


def solution(mesh):
    placed = (
        P(("row", "col"), None),
        P("row", "col", None, None, None),
        P("row", "col", None),
        P("row", "col", None),
        P("row", "col"),
        P(),
        P(),
        P(),
        P(),
        P(),
        P(),
        P(),
        P(),
        P(),
        P(),
        P(),
        P(),
        P(),
        P(),
        P(("row", "col"), None),
    )
    return jax.shard_map(
        per_device,
        mesh=mesh,
        in_specs=placed,
        out_specs=(
            P(("row", "col"), None),
            P(("row", "col"), None),
            P(),
            P(),
            P(),
            P(),
            P(),
            P(),
            P(),
            P(),
            P(),
            P(),
            P(),
            P(),
            P(),
            P(),
        ),
        check_vma=False,
    )
```

profile of v0, /device:TPU:0, one launch (start us, length us, event | category | flops | bytes accessed | tf_op | source)
XLA Modules:
  0.0 1398.2 jit_solution(17185425207712821760)
XLA Ops:
  9.5 41.4 %all-gather.9.cloned.1.call-done = f32[2048,128]{1,0:T(8,128)} async-done(((f32[128,128]{1,0:T(8,128)}), f32[2048,128]{1,0:T(8,128)}) %all-gather.9.cloned.1.call-update) | async-done | bytes 1048592 | tf_op jit(solution)/shard_map/all_gather | solution.py:104
  59.8 9.3 reduce-scatter.15.cloned.1.call-done
  69.1 40.1 %all-gather.11.cloned.1.call-done = f32[2048,128]{1,0:T(8,128)} async-done(((f32[128,128]{1,0:T(8,128)}), f32[2048,128]{1,0:T(8,128)}) %all-gather.11.cloned.1.call-update) | async-done | bytes 1048592 | tf_op jit(solution)/shard_map/all_gather | solution.py:104
  127.4 39.9 %all-gather.13.cloned.1.call-done = f32[2048,128]{1,0:T(8,128)} async-done(((f32[128,128]{1,0:T(8,128)}), f32[2048,128]{1,0:T(8,128)}) %all-gather.13.cloned.1.call-update) | async-done | bytes 1048592 | tf_op jit(solution)/shard_map/all_gather | solution.py:104
  176.1 9.3 reduce-scatter.19.cloned.1.call-done
  185.4 40.1 %all-gather.15.cloned.1.call-done = f32[2048,128]{1,0:T(8,128)} async-done(((f32[128,128]{1,0:T(8,128)}), f32[2048,128]{1,0:T(8,128)}) %all-gather.15.cloned.1.call-update) | async-done | bytes 1048592 | tf_op jit(solution)/shard_map/all_gather | solution.py:104
  234.3 9.3 reduce-scatter.21.cloned.1.call-done
  243.7 40.1 %all-gather.17.cloned.1.call-done = f32[2048,128]{1,0:T(8,128)} async-done(((f32[128,128]{1,0:T(8,128)}), f32[2048,128]{1,0:T(8,128)}) %all-gather.17.cloned.1.call-update) | async-done | bytes 1048592 | tf_op jit(solution)/shard_map/all_gather | solution.py:104
  301.9 40.1 %all-gather.19.cloned.1.call-done = f32[2048,128]{1,0:T(8,128)} async-done(((f32[128,128]{1,0:T(8,128)}), f32[2048,128]{1,0:T(8,128)}) %all-gather.19.cloned.1.call-update) | async-done | bytes 1048592 | tf_op jit(solution)/shard_map/all_gather | solution.py:104
  366.4 33.8 %all-gather.21.cloned.1.call-done = f32[2048,128]{1,0:T(8,128)} async-done(((f32[128,128]{1,0:T(8,128)}), f32[2048,128]{1,0:T(8,128)}) %all-gather.21.cloned.1.call-update) | async-done | bytes 1048592 | tf_op jit(solution)/shard_map/all_gather | solution.py:104
  424.0 10.8 fusion.10
  434.9 14.4 %fusion.197 = (f32[128,8,512]{2,0,1:T(8,128)}, f32[128,8,512]{2,0,1:T(8,128)}, f32[128,8,512]{2,0,1:T(8,128)}) fusion(f32[128,8,1536]{2,0,1:T(8,128)S(1)} %fusion.10), kind=kLoop, calls=%fused_computation.285 | loop fusion | bytes 12582912 | tf_op jit(solution)/shard_map/jvp()/slice | solution.py:42
  474.8 9.8 multiply_reduce_fusion.1
  488.8 10.2 convolution_bitcast_fusion.3
  519.2 9.3 fusion.2
  549.4 14.6 %fusion.199 = (f32[1024]{0:T(1024)}, f32[128,8,1024]{2,0,1:T(8,128)S(1)}) fusion(f32[128,8,1024]{2,0,1:T(8,128)} %copy-done.9, f32[1024,512]{1,0:T(8,128)} %param.36, f32[128,1,512]{2,0,1:T(8,128)} %bitcast.328, f32[128,7,512]{2,0,1:T(8,128)S(1)} %multiply_add_fusion.3, f32[128,8,1024]{2,0,1:T(8,128)} %copy-done.7, f32[1024]{0:T(1024)S(1)} %copy-done.43), kind=kOutput, calls=%fused_computation.287 | convolution fusion | flops 6458702848 | bytes 16785408 | tf_op jit(solution)/shard_map/transpose(jvp(nte,ed->ntd))/dot_general | solution.py:57
  587.0 16.1 %multiply_reduce_fusion = (f32[128,8,8]{2,1,0:T(8,128)}, f32[128,8,8,8]{2,3,1,0:T(8,128)}) fusion(f32[128,8,8]{2,1,0:T(8,128)} %multiply_divide_fusion, f32[128,8,8]{2,1,0:T(8,128)} %copy-done.20, f32[128,8,8,8]{2,3,1,0:T(8,128)} %copy-done.10, f32[128,8,64,8]{2,3,1,0:T(8,128)} %copy.74, f32[128,8,8,64]{3,1,2,0:T(8,128)} %copy.69), kind=kOutput, calls=%fused_computation.25 | convolution fusion | flops 50651136 | bytes 4816896 | tf_op jit(solution)/shard_map/transpose(jvp(nhqk,nkhe->nqhe))/dot_general | solution.py:48
  605.0 12.5 convolution_bitcast_fusion
  617.5 14.7 %convolution_bitcast_fusion.1 = f32[128,8,8,64]{3,1,2,0:T(8,128)} fusion(f32[128,8,8,64]{3,1,2,0:T(8,128)} %copy.67, f32[128,8,8,8]{2,3,1,0:T(8,128)} %get-tuple-element.59, f32[128,8,8]{2,1,0:T(8,128)} %copy-done.39, f32[128,8,8]{2,1,0:T(8,128)S(1)} %copy-done.30, f32[128,8,8]{2,1,0:T(8,128)S(1)} %copy-done.21, f32[128,8,8,8]{2,3,1,0:T(8,128)} %copy-done.10), kind=kOutput, calls=%fused_computation.49 | convolution fusion | flops 50724864 | bytes 4816896 | tf_op jit(solution)/shard_map/transpose(jvp(nqhe,nkhe->nhqk))/dot_general | solution.py:46
  632.2 13.5 convolution_bitcast_fusion.2
  659.9 24.2 %fusion.194 = (f32[512]{0:T(512)}, f32[128,8]{0,1:T(8,128)S(1)}, f32[128,8,512]{2,0,1:T(8,128)S(1)}) fusion(f32[512]{0:T(512)S(1)} %copy-done.55, f32[128,8]{0,1:T(8,128)S(1)} %broadcast_multiply_fusion.1, f32[128,8,512]{2,0,1:T(8,128)} %copy-done.3, f32[512]{0:T(512)S(1)} %copy-done.42, f32[512,1536]{1,0:T(8,128)S(1)} %copy-done, ...), kind=kOutput, calls=%fused_computation.282 | convolution fusion | flops 9669965824 | bytes 13645824 | tf_op jit(solution)/shard_map/transpose(jvp(ntd,de->nte))/dot_general | solution.py:40
  705.3 57.6 %reduce-scatter.29.cloned.1.call-done = f32[128,128]{1,0:T(8,128)} async-done(((f32[2048,128]{1,0:T(8,128)}), f32[128,128]{1,0:T(8,128)}) %reduce-scatter.29.cloned.1.call-update) | async-done | bytes 65552 | tf_op jit(solution)/shard_map/reduce_scatter | solution.py:197
  777.6 56.5 %reduce-scatter.31.cloned.1.call-done = f32[128,128]{1,0:T(8,128)} async-done(((f32[2048,128]{1,0:T(8,128)}), f32[128,128]{1,0:T(8,128)}) %reduce-scatter.31.cloned.1.call-update) | async-done | bytes 65552 | tf_op jit(solution)/shard_map/reduce_scatter | solution.py:197
  848.9 56.5 %reduce-scatter.33.cloned.1.call-done = f32[128,128]{1,0:T(8,128)} async-done(((f32[2048,128]{1,0:T(8,128)}), f32[128,128]{1,0:T(8,128)}) %reduce-scatter.33.cloned.1.call-update) | async-done | bytes 65552 | tf_op jit(solution)/shard_map/reduce_scatter | solution.py:197
  920.1 56.5 %reduce-scatter.35.cloned.1.call-done = f32[128,128]{1,0:T(8,128)} async-done(((f32[2048,128]{1,0:T(8,128)}), f32[128,128]{1,0:T(8,128)}) %reduce-scatter.35.cloned.1.call-update) | async-done | bytes 65552 | tf_op jit(solution)/shard_map/reduce_scatter | solution.py:197
  991.8 56.4 %reduce-scatter.37.cloned.1.call-done = f32[128,128]{1,0:T(8,128)} async-done(((f32[2048,128]{1,0:T(8,128)}), f32[128,128]{1,0:T(8,128)}) %reduce-scatter.37.cloned.1.call-update) | async-done | bytes 65552 | tf_op jit(solution)/shard_map/reduce_scatter | solution.py:197
  1062.9 11.2 fusion.24
  1074.1 45.4 %reduce-scatter.39.cloned.1.call-done = f32[128,128]{1,0:T(8,128)} async-done(((f32[2048,128]{1,0:T(8,128)}), f32[128,128]{1,0:T(8,128)}) %reduce-scatter.39.cloned.1.call-update) | async-done | bytes 65552 | tf_op jit(solution)/shard_map/reduce_scatter | solution.py:197
  1144.3 10.2 convolution_bitcast_fusion.4
  1154.7 22.1 %fusion.8 = f32[512,1536]{1,0:T(8,128)} fusion(f32[128,8,512]{0,2,1:T(8,128)S(1)} %bitcast.343, f32[128,8,512]{0,2,1:T(8,128)S(1)} %bitcast.341, f32[128,8,512]{0,2,1:T(8,128)S(1)} %bitcast.339, f32[512]{0:T(512)S(1)} %copy-done.69, f32[512]{0:T(512)S(1)} %copy-done.56, f32[128,8]{0,1:T(8,128)S(1)} %copy-done.46, f32[128,8,512]{2,0,1:T(8,128)S(1)} %copy-done.5, ...), kind=kOutput, calls=%fused_computation.42 | convolution fusion | flops 9669443584 | bytes 11548672 | tf_op jit(solution)/shard_map/transpose(jvp(ntd,de->nte))/dot_general | solution.py:40
  1180.1 41.8 %all-reduce.5 = (f32[512]{0:T(512)}, f32[512]{0:T(512)}, f32[512]{0:T(512)}, f32[512]{0:T(512)}, f32[512]{0:T(512)}, /*index=5*/f32[512]{0:T(512)}, f32[1024]{0:T(1024)}, f32[512]{0:T(512)}, f32[512]{0:T(512)}) all-reduce(f32[512]{0:T(512)S(1)} %copy-done.60, f32[512]{0:T(512)S(1)} %copy-done.59, ...), channel_id=1, replica_groups=mesh['row'=16,'col'=2] {'row','col'}, use_global_device_ids=true, to_apply=%region_30.0 | all-reduce | flops 5120 | bytes 40960 | tf_op jit(solution)/shard_map/psum | solution.py:200
  1229.5 152.0 %all-reduce.9.cloned.1.call-done = (f32[128,512]{1,0:T(8,128)}, f32[512,1536]{1,0:T(8,128)}, f32[512,512]{1,0:T(8,128)}, f32[512,1024]{1,0:T(8,128)}, f32[1024,512]{1,0:T(8,128)}) async-done(((f32[128,512]{1,0:T(8,128)}, f32[512,1536]{1,0:T(8,128)}, f32[512,512]{1,0:T(8,128)}, f32[512,1024]{1,0:T(8,128)}, f32[1024,512]{1,0:T(8,128)}), (f32[128,512]{1,0:T(8,128)}, f32[512,1536]{1,0:T(8,128)}, ...) | async-done | bytes 8650768 | tf_op jit(solution)/shard_map/psum | solution.py:200
  (345 shorter events, 361.8 us)
Async XLA Ops:
  7.2 416.8 %copy-start = (f32[512,1536]{1,0:T(8,128)S(1)}, f32[512,1536]{1,0:T(8,128)}, u32[]{:S(2)}) copy-start(f32[512,1536]{1,0:T(8,128)} %param.29) | copy-start | bytes 9437188
  7.2 162.6 %copy-start.6 = (f32[1,1,4,128,128]{4,3,2,1,0:T(8,128)S(1)}, f32[1,1,4,128,128]{4,3,2,1,0:T(8,128)}, u32[]{:S(2)}) copy-start(f32[1,1,4,128,128]{4,3,2,1,0:T(8,128)} %param.21) | copy-start | bytes 786436
  7.2 108.6 %copy-start.52 = (s32[1,1,4]{2,1,0:T(1,128)S(1)}, s32[1,1,4]{2,1,0:T(1,128)}, u32[]{:S(2)}) copy-start(s32[1,1,4]{2,1,0:T(1,128)} %param.22) | copy-start | bytes 52
  7.2 43.7 %all-gather.9.cloned.1.call-start = ((), (), s32[]{:S(2)}) async-start(), calls=%async_computation.14 | async-start | bytes 1114112 | tf_op jit(solution)/shard_map/all_gather | solution.py:104
  8.0 61.1 %reduce-scatter.15.cloned.1.call-start = ((), (), s32[]{:S(2)}) async-start(), calls=%async_computation.15 | async-start | bytes 196608 | tf_op jit(solution)/shard_map/reduce_scatter | solution.py:113
  59.7 49.5 %all-gather.11.cloned.1.call-start = ((), (), s32[]{:S(2)}) async-start(), calls=%async_computation.16 | async-start | bytes 1114112 | tf_op jit(solution)/shard_map/all_gather | solution.py:104
  69.1 58.3 %reduce-scatter.17.cloned.1.call-start = ((), (), s32[]{:S(2)}) async-start(), calls=%async_computation.17 | async-start | bytes 196608 | tf_op jit(solution)/shard_map/reduce_scatter | solution.py:113
  118.0 49.3 %all-gather.13.cloned.1.call-start = ((), (), s32[]{:S(2)}) async-start(), calls=%async_computation.18 | async-start | bytes 1114112 | tf_op jit(solution)/shard_map/all_gather | solution.py:104
  127.3 58.0 %reduce-scatter.19.cloned.1.call-start = ((), (), s32[]{:S(2)}) async-start(), calls=%async_computation.19 | async-start | bytes 196608 | tf_op jit(solution)/shard_map/reduce_scatter | solution.py:113
  176.0 184.7 %copy-start.40 = (f32[128,128]{1,0:T(8,128)S(1)}, f32[128,128]{1,0:T(8,128)}, u32[]{:S(2)}) copy-start(f32[128,128]{1,0:T(8,128)} %param.20) | copy-start | bytes 196612
  176.0 185.3 %copy-start.41 = (f32[128,128]{1,0:T(8,128)S(1)}, f32[128,128]{1,0:T(8,128)}, u32[]{:S(2)}) copy-start(f32[128,128]{1,0:T(8,128)} %reduce-scatter.15.cloned.1.call-done) | copy-start | bytes 196612
  176.1 49.5 %all-gather.15.cloned.1.call-start = ((), (), s32[]{:S(2)}) async-start(), calls=%async_computation.20 | async-start | bytes 1114112 | tf_op jit(solution)/shard_map/all_gather | solution.py:104
  185.4 58.2 %reduce-scatter.21.cloned.1.call-start = ((), (), s32[]{:S(2)}) async-start(), calls=%async_computation.21 | async-start | bytes 196608 | tf_op jit(solution)/shard_map/reduce_scatter | solution.py:113
  234.3 49.5 %all-gather.17.cloned.1.call-start = ((), (), s32[]{:S(2)}) async-start(), calls=%async_computation.22 | async-start | bytes 1114112 | tf_op jit(solution)/shard_map/all_gather | solution.py:104
  243.6 58.2 %reduce-scatter.23.cloned.1.call-start = ((), (), s32[]{:S(2)}) async-start(), calls=%async_computation.23 | async-start | bytes 196608 | tf_op jit(solution)/shard_map/reduce_scatter | solution.py:113
  286.2 133.5 %copy-start.42 = (f32[512]{0:T(512)S(1)}, f32[512]{0:T(512)}, u32[]{:S(2)}) copy-start(f32[512]{0:T(512)} %param.26) | copy-start | bytes 6148
  292.5 49.5 %all-gather.19.cloned.1.call-start = ((), (), s32[]{:S(2)}) async-start(), calls=%async_computation.24 | async-start | bytes 1114112 | tf_op jit(solution)/shard_map/all_gather | solution.py:104
  301.8 58.2 %reduce-scatter.25.cloned.1.call-start = ((), (), s32[]{:S(2)}) async-start(), calls=%async_computation.25 | async-start | bytes 196608 | tf_op jit(solution)/shard_map/reduce_scatter | solution.py:113
  350.7 49.5 %all-gather.21.cloned.1.call-start = ((), (), s32[]{:S(2)}) async-start(), calls=%async_computation.26 | async-start | bytes 1114112 | tf_op jit(solution)/shard_map/all_gather | solution.py:104
  360.0 58.2 %reduce-scatter.27.cloned.1.call-start = ((), (), s32[]{:S(2)}) async-start(), calls=%async_computation.27 | async-start | bytes 196608 | tf_op jit(solution)/shard_map/reduce_scatter | solution.py:113
  361.9 62.1 %copy-start.55 = (f32[512]{0:T(512)S(1)}, f32[512]{0:T(512)}, u32[]{:S(2)}) copy-start(f32[512]{0:T(512)} %param.27) | copy-start | bytes 6148
  361.9 62.1 %copy-start.68 = (f32[512]{0:T(512)S(1)}, f32[512]{0:T(512)}, u32[]{:S(2)}) copy-start(f32[512]{0:T(512)} %param.28) | copy-start | bytes 6148
  408.9 354.0 %reduce-scatter.29.cloned.1.call-start = ((), (), s32[]{:S(2)}) async-start(), calls=%async_computation.28 | async-start | bytes 1114112 | tf_op jit(solution)/shard_map/reduce_scatter | solution.py:197
  424.0 262.0 %copy-start.45 = (f32[128,8]{0,1:T(8,128)}, f32[128,8]{0,1:T(8,128)S(1)}, u32[]{:S(2)}) copy-start(f32[128,8]{0,1:T(8,128)S(1)} %fusion.126) | copy-start | bytes 12292
  511.1 62.3 %copy-start.47 = (f32[128,8]{0,1:T(8,128)}, f32[128,8]{0,1:T(8,128)S(1)}, u32[]{:S(2)}) copy-start(f32[128,8]{0,1:T(8,128)S(1)} %fusion.127) | copy-start | bytes 12292
  705.3 128.9 %reduce-scatter.31.cloned.1.call-start = ((), (), s32[]{:S(2)}) async-start(), calls=%async_computation.29 | async-start | bytes 1114112 | tf_op jit(solution)/shard_map/reduce_scatter | solution.py:197
  777.6 127.8 %reduce-scatter.33.cloned.1.call-start = ((), (), s32[]{:S(2)}) async-start(), calls=%async_computation.30 | async-start | bytes 1114112 | tf_op jit(solution)/shard_map/reduce_scatter | solution.py:197
  848.8 127.8 %reduce-scatter.35.cloned.1.call-start = ((), (), s32[]{:S(2)}) async-start(), calls=%async_computation.31 | async-start | bytes 1114112 | tf_op jit(solution)/shard_map/reduce_scatter | solution.py:197
  920.1 128.1 %reduce-scatter.37.cloned.1.call-start = ((), (), s32[]{:S(2)}) async-start(), calls=%async_computation.32 | async-start | bytes 1114112 | tf_op jit(solution)/shard_map/reduce_scatter | solution.py:197
  991.7 127.8 %reduce-scatter.39.cloned.1.call-start = ((), (), s32[]{:S(2)}) async-start(), calls=%async_computation.33 | async-start | bytes 1114112 | tf_op jit(solution)/shard_map/reduce_scatter | solution.py:197
  1062.9 165.1 %reduce-scatter.41.cloned.1.call-start = ((), (), s32[]{:S(2)}) async-start(), calls=%async_computation.34 | async-start | bytes 1114112 | tf_op jit(solution)/shard_map/reduce_scatter | solution.py:197
  1133.2 248.3 %all-reduce.9.cloned.1.call-start = ((), (), s32[]{:S(2)}) async-start(), calls=%async_computation.35 | async-start | bytes 17301504 | tf_op jit(solution)/shard_map/psum | solution.py:200
  (60 other events, 467.9 us)
Sparse Core Ops, SparseCore 0:
  10.2 40.6 all-gather.8
  59.8 9.1 reduce-scatter.14
  71.2 37.9 all-gather.10
  118.1 9.1 reduce-scatter.16
  129.3 37.9 all-gather.12
  176.2 9.1 reduce-scatter.18
  187.5 37.9 all-gather.14
  234.4 9.1 reduce-scatter.20
  245.7 37.9 all-gather.16
  292.6 9.1 reduce-scatter.22
  304.0 37.9 all-gather.18
  350.8 9.1 reduce-scatter.24
  362.2 37.9 all-gather.20
  409.0 9.1 reduce-scatter.26
  705.4 57.4 reduce-scatter.28
  777.7 56.4 reduce-scatter.30
  849.0 56.3 reduce-scatter.32
  920.2 56.4 reduce-scatter.34
  991.9 56.2 reduce-scatter.36
  1063.0 56.4 reduce-scatter.38
  1133.3 56.4 reduce-scatter.40
  1198.5 183.0 all-reduce.8
where the time goes:
time: 1410 us; the launch traced here: 1400 us
  waiting for transfers between devices  819 us (58%)
  matrix products  292 us (21%)
  local copies, waits for them, and re-layouts  160 us (11%)
  blocking collectives  76.8 us (5%)
  other arithmetic  31.6 us (2%)
  between operations  16.6 us (1%)
    reduce_scatter x7, waiting for transfers between devices, per_device(): lax.psum_scatter(partial_value, 'row', scatter_dimension=0, tiled=True)  329 us
    all_gather x7, waiting for transfers between devices, per_device(): lax.all_gather(field, 'row', axis=0, tiled=True)  276 us
    psum x1, waiting for transfers between devices, per_device(): lax.psum((grad_w_input, grad_bias_input, grad_gain_attn, grad_shift_attn,...  152 us
    reduce_scatter x7, waiting for transfers between devices, per_device(): lax.psum_scatter(forward_partial_value, 'col', scatter_dimension=0, tiled...  61.6 us
    dot_general x3, matrix products, node_tail(): projected = jnp.einsum('ntd,de->nte', normed, w_heads, precision=exact)  57.1 us
    psum x1, blocking collectives, per_device(): lax.psum((grad_w_input, grad_bias_input, grad_gain_attn, grad_shift_attn,...  41.8 us
    dot_general x3, matrix products, node_tail(): jnp.einsum('nhqk,nkhe->nqhe', attention, value_rows, precision=exact)  39.7 us
    dot_general x3, matrix products, node_tail(): jnp.einsum('nqhe,nkhe->nhqk', queries, key_rows, precision=exact)  37 us
  transfers between devices with their start and end apart: 22, of which 21 were waited for; matrix products, arithmetic and copies ran while one was open for 5% of the time, Pallas kernels for 0%

commit v1 on v0

--- a/solution.py
+++ b/solution.py
@@ -1,8 +1,11 @@
+import functools
 import math
 
 import jax
 import jax.numpy as jnp
 from jax import lax
+from jax.experimental import pallas as pl
+from jax.experimental.pallas import tpu as pltpu
 from jax.sharding import PartitionSpec as P
 
 HEADS = 8
@@ -11,6 +14,129 @@
 
 
 exact = lax.Precision.HIGHEST
+near = lax.Precision.HIGH
+AXES = ("row", "col")
+LANES = 128
+PIECE = 4
+UNROLL = 4
+
+
+def block_list(meta_ref, source, taken, given, slots, n_col, row_blocks):
+    def tile(position, live):
+        row, col = position // n_col, position % n_col
+        count = meta_ref[position, 2 * slots]
+        for slot in range(slots):
+            source[live] = position * slots + slot
+            given[live] = row * row_blocks + meta_ref[position, slot]
+            taken[live] = meta_ref[position, slots + slot] * n_col + col
+            live = live + jnp.where(slot < count, 1, 0)
+        return live
+
+    tiles = meta_ref.shape[0]
+    live = lax.fori_loop(0, tiles, tile, jnp.int32(0))
+    for extra in range(UNROLL):
+        source[live + extra] = 0
+        given[live + extra] = tiles
+        taken[live + extra] = tiles
+    return (live + UNROLL - 1) // UNROLL
+
+
+def walk_kernel(
+    forward, hops, slots, n_col, row_blocks, meta_ref, field_ref, values_ref, out_ref, upper, lower, total, state, source, taken, given
+):
+    if forward:
+        steps = block_list(meta_ref, source, taken, given, slots, n_col, row_blocks)
+    else:
+        steps = block_list(meta_ref, source, given, taken, slots, n_col, row_blocks)
+    blocks = field_ref.shape[0]
+
+    def split(step, _):
+        for inner in range(UNROLL):
+            place = step * UNROLL + inner
+            block = values_ref[source[place]]
+            rounded = block.astype(jnp.bfloat16)
+            upper[place] = rounded
+            lower[place] = (block - rounded.astype(jnp.float32)).astype(jnp.bfloat16)
+        return 0
+
+    lax.fori_loop(0, steps, split, 0)
+    state[blocks] = jnp.zeros_like(state[blocks])
+    is_top = lax.broadcasted_iota(jnp.int32, (blocks, 2 * PIECE, LANES), 1) < PIECE
+
+    def keep(field):
+        doubled = jnp.concatenate([field, field], axis=1)
+        rounded = doubled.astype(jnp.bfloat16).astype(jnp.float32)
+        state[:blocks] = jnp.where(is_top, rounded, doubled - rounded)
+
+    def apply():
+        total[...] = jnp.zeros_like(total)
+
+        def some(step, _):
+            products = []
+            for inner in range(UNROLL):
+                place = step * UNROLL + inner
+                rows = state[taken[place]].astype(jnp.bfloat16)
+                axis = 1 if forward else 0
+                dims = (((1,), (axis,)), ((), ()))
+                products.append(
+                    lax.dot_general(rows, upper[place], dims, preferred_element_type=jnp.float32)
+                    + lax.dot_general(rows, lower[place], dims, preferred_element_type=jnp.float32)
+                )
+            for inner in range(UNROLL):
+                target = given[step * UNROLL + inner]
+                total[target] = total[target] + products[inner]
+            return 0
+
+        lax.fori_loop(0, steps, some, 0)
+        summed = total[:blocks]
+        return summed[:, :PIECE] + summed[:, PIECE:]
+
+    if forward:
+        field = field_ref[:, :PIECE]
+        out_ref[:, :PIECE] = field
+        keep(field)
+        for hop in range(1, hops + 1):
+            field = apply()
+            out_ref[:, hop * PIECE : (hop + 1) * PIECE] = field
+            if hop < hops:
+                keep(field)
+    else:
+        field = field_ref[:, hops * PIECE :]
+        for hop in range(hops - 1, -1, -1):
+            keep(field)
+            field = apply()
+            if hop > 0:
+                field = field + field_ref[:, hop * PIECE : (hop + 1) * PIECE]
+        out_ref[:, :PIECE] = field
+        out_ref[:, PIECE:] = field
+
+
+def walk(forward, meta, field, values, n_col, row_blocks):
+    blocks = field.shape[0]
+    slots = values.shape[0] // meta.shape[0]
+    room = values.shape[0] + UNROLL
+    out_rows = (HOPS + 1) * PIECE if forward else 2 * PIECE
+    return pl.pallas_call(
+        functools.partial(walk_kernel, forward, HOPS, slots, n_col, row_blocks),
+        out_shape=jax.ShapeDtypeStruct((blocks, out_rows, LANES), jnp.float32),
+        in_specs=[
+            pl.BlockSpec(memory_space=pltpu.SMEM),
+            pl.BlockSpec(memory_space=pltpu.VMEM),
+            pl.BlockSpec(memory_space=pltpu.VMEM),
+        ],
+        out_specs=pl.BlockSpec(memory_space=pltpu.VMEM),
+        scratch_shapes=[
+            pltpu.VMEM((room, LANES, LANES), jnp.bfloat16),
+            pltpu.VMEM((room, LANES, LANES), jnp.bfloat16),
+            pltpu.VMEM((blocks + 1, 2 * PIECE, LANES), jnp.float32),
+            pltpu.VMEM((blocks + 1, 2 * PIECE, LANES), jnp.float32),
+            pltpu.SMEM((room,), jnp.int32),
+            pltpu.SMEM((room,), jnp.int32),
+            pltpu.SMEM((room,), jnp.int32),
+        ],
+        compiler_params=pltpu.CompilerParams(vmem_limit_bytes=48 << 20),
+        name="walk_forward" if forward else "walk_backward",
+    )(meta, field, values)
 
 
 def layer_norm(values, gain, shift):
@@ -37,28 +163,28 @@
 ):
     node_count, token_count, columns = start.shape
     normed = layer_norm(start, gain_attn, shift_attn)
-    projected = jnp.einsum("ntd,de->nte", normed, w_heads, precision=exact)
+    projected = jnp.einsum("ntd,de->nte", normed, w_heads, precision=near)
     queries = projected[..., :columns].reshape(node_count, token_count, HEADS, HEAD_DIM)
     key_rows = projected[..., columns : 2 * columns].reshape(
         node_count, token_count, HEADS, HEAD_DIM
     )
     value_rows = projected[..., 2 * columns :].reshape(node_count, token_count, HEADS, HEAD_DIM)
-    scores = jnp.einsum("nqhe,nkhe->nhqk", queries, key_rows, precision=exact) / math.sqrt(HEAD_DIM)
+    scores = jnp.einsum("nqhe,nkhe->nhqk", queries, key_rows, precision=near) / math.sqrt(HEAD_DIM)
     attention = jax.nn.softmax(scores, axis=-1)
-    mixed = jnp.einsum("nhqk,nkhe->nqhe", attention, value_rows, precision=exact).reshape(
+    mixed = jnp.einsum("nhqk,nkhe->nqhe", attention, value_rows, precision=near).reshape(
         node_count, token_count, columns
     )
-    middle = start + jnp.einsum("ntd,de->nte", mixed, w_merge, precision=exact) + bias_merge
+    middle = start + jnp.einsum("ntd,de->nte", mixed, w_merge, precision=near) + bias_merge
     normed_two = layer_norm(middle, gain_ffn, shift_ffn)
     activated = jax.nn.gelu(
-        jnp.einsum("ntd,de->nte", normed_two, w_expand, precision=exact) + bias_expand,
+        jnp.einsum("ntd,de->nte", normed_two, w_expand, precision=near) + bias_expand,
         approximate=False,
     )
-    final = middle + jnp.einsum("nte,ed->ntd", activated, w_reduce, precision=exact) + bias_reduce
+    final = middle + jnp.einsum("nte,ed->ntd", activated, w_reduce, precision=near) + bias_reduce
     center = final[:, 0]
     others = final[:, 1:]
-    weights = jax.nn.softmax(jnp.einsum("nkd,d->nk", others, readout, precision=exact), axis=-1)
-    return center + jnp.einsum("nk,nkd->nd", weights, others, precision=exact)
+    weights = jax.nn.softmax(jnp.einsum("nkd,d->nk", others, readout, precision=near), axis=-1)
+    return center + jnp.einsum("nk,nkd->nd", weights, others, precision=near)
 
 
 def per_device(
@@ -97,22 +223,48 @@
     col_table = (col_ids[:, None] == jnp.arange(col_blocks)[None, :]).astype(jnp.float32) * is_live[
         :, None
     ]
-    hop_list = [node_features]
-    for hop_index in range(HOPS):
-        field = hop_list[-1]
-        forward_columns = field.shape[1]
-        forward_gathered = lax.all_gather(field, "row", axis=0, tiled=True).reshape(
-            col_blocks, block_size, forward_columns
+    devices = lax.axis_size("row") * lax.axis_size("col")
+    whole = (
+        block_size == LANES
+        and node_count == LANES
+        and node_features.shape[1] == PIECE * devices
+        and devices * values.size * 4 <= 16 << 20
+    )
+    if whole:
+        n_col = lax.axis_size("col")
+        everything = lax.all_gather(values, AXES, axis=0, tiled=True)
+        places = jnp.concatenate([row_ids, col_ids, block_count[0]]).astype(jnp.float32)
+        note = jnp.zeros((PIECE, LANES), jnp.float32).at[0, : places.shape[0]].set(places)
+        sent = jnp.concatenate(
+            [
+                node_features.T.reshape(devices, PIECE, LANES),
+                jnp.broadcast_to(note[None], (devices, PIECE, LANES)),
+            ],
+            axis=1,
         )
-        forward_picked = forward_gathered[col_ids]
-        forward_products = jnp.einsum("bij,bjw->biw", values, forward_picked, precision=exact)
-        forward_partial_value = jnp.einsum(
-            "br,biw->riw", row_table, forward_products, precision=exact
-        ).reshape(row_blocks * block_size, forward_columns)
-        hop_list.append(
-            lax.psum_scatter(forward_partial_value, "col", scatter_dimension=0, tiled=True)
-        )
-    stacked = jnp.stack(hop_list, axis=1)
+        taken = lax.all_to_all(sent, AXES, 0, 0, tiled=True)
+        meta = taken[:, PIECE, : places.shape[0]].astype(jnp.int32)
+        walked = walk(True, meta, taken, everything, n_col, row_blocks)
+        walked = lax.all_to_all(walked, AXES, 0, 0, tiled=True)
+        stacked = walked.reshape(devices, HOPS + 1, PIECE, LANES).transpose(3, 1, 0, 2)
+        stacked = stacked.reshape(LANES, HOPS + 1, devices * PIECE)
+    else:
+        hop_list = [node_features]
+        for hop_index in range(HOPS):
+            field = hop_list[-1]
+            forward_columns = field.shape[1]
+            forward_gathered = lax.all_gather(field, "row", axis=0, tiled=True).reshape(
+                col_blocks, block_size, forward_columns
+            )
+            forward_picked = forward_gathered[col_ids]
+            forward_products = jnp.einsum("bij,bjw->biw", values, forward_picked, precision=exact)
+            forward_partial_value = jnp.einsum(
+                "br,biw->riw", row_table, forward_products, precision=exact
+            ).reshape(row_blocks * block_size, forward_columns)
+            hop_list.append(
+                lax.psum_scatter(forward_partial_value, "col", scatter_dimension=0, tiled=True)
+            )
+        stacked = jnp.stack(hop_list, axis=1)
 
     def local_layer(
         stacked_hops,
@@ -131,7 +283,7 @@
         bias_reduce,
         readout,
     ):
-        start = jnp.einsum("ntf,fd->ntd", stacked_hops, w_input, precision=exact) + bias_input
+        start = jnp.einsum("ntf,fd->ntd", stacked_hops, w_input, precision=near) + bias_input
         return node_tail(
             start,
             gain_attn,
@@ -183,20 +335,28 @@
         grad_bias_reduce,
         grad_readout,
     ) = pullback(cotangent)
-    carried = grad_hops[:, HOPS]
-    for hop_index in range(HOPS - 1, -1, -1):
-        columns = carried.shape[1]
-        gathered = lax.all_gather(carried, "col", axis=0, tiled=True).reshape(
-            row_blocks, block_size, columns
-        )
-        picked = gathered[row_ids]
-        products = jnp.einsum("bji,bjw->biw", values, picked, precision=exact)
-        partial_value = jnp.einsum("bc,biw->ciw", col_table, products, precision=exact).reshape(
-            col_blocks * block_size, columns
-        )
-        carried = grad_hops[:, hop_index] + lax.psum_scatter(
-            partial_value, "row", scatter_dimension=0, tiled=True
-        )
+    if whole:
+        sent = grad_hops.reshape(LANES, HOPS + 1, devices, PIECE).transpose(2, 1, 3, 0)
+        sent = sent.reshape(devices, (HOPS + 1) * PIECE, LANES)
+        back = lax.all_to_all(sent, AXES, 0, 0, tiled=True)
+        back = walk(False, meta, back, everything, n_col, row_blocks)
+        back = lax.all_to_all(back, AXES, 0, 0, tiled=True)[:, :PIECE]
+        carried = grad_hops[:, 0] + back.reshape(devices * PIECE, LANES).T
+    else:
+        carried = grad_hops[:, HOPS]
+        for hop_index in range(HOPS - 1, -1, -1):
+            columns = carried.shape[1]
+            gathered = lax.all_gather(carried, "col", axis=0, tiled=True).reshape(
+                row_blocks, block_size, columns
+            )
+            picked = gathered[row_ids]
+            products = jnp.einsum("bji,bjw->biw", values, picked, precision=exact)
+            partial_value = jnp.einsum("bc,biw->ciw", col_table, products, precision=exact).reshape(
+                col_blocks * block_size, columns
+            )
+            carried = grad_hops[:, hop_index] + lax.psum_scatter(
+                partial_value, "row", scatter_dimension=0, tiled=True
+            )
     summed = lax.psum(
         (
             grad_w_input,

time: 1410 us -> 583 us (0.41)
  waiting for transfers between devices: 819 us -> 173 us
  matrix products: 292 us -> 146 us
  local copies, waits for them, and re-layouts: 160 us -> 75.9 us
  Pallas kernels: 0 us -> 54.2 us
    reduce_scatter x14 -> x0, waiting for transfers between devices: 391 us -> none  [the longest x7 329 us: per_device(): lax.psum_scatter(partial_value, 'row', scatter_dimension=0, tiled=True)]
    all_gather x7 -> x1, waiting for transfers between devices: 276 us -> 64.7 us  [per_device(): everything = lax.all_gather(values, AXES, axis=0, tiled=True)]
    dot_general x53 -> x25, matrix products: 292 us -> 146 us  [the longest x3 32.4 us: node_tail(): projected = jnp.einsum('ntd,de->nte', normed, w_heads, precision=near)]
    psum x1, waiting for transfers between devices: 152 us -> 87.9 us  [per_device(): lax.psum((grad_w_input, grad_bias_input, grad_gain_attn, grad_shift_attn,...]
    pallas_call x0 -> x2, Pallas kernels: none -> 54.2 us  [walk(): pl.pallas_call(functools.partial(walk_kernel, forward, HOPS, slots, n_col...]
    dot_general x30 -> x2, local copies, waits for them, and re-layouts: 39.3 us -> 1.26 us  [the longest x1 1.2 us: node_tail(): jnp.einsum('nkd,d->nk', others, readout, precision=near)]
    all_gather x7 -> x0, blocking collectives: 35 us -> none  [per_device(): lax.all_gather(carried, 'col', axis=0, tiled=True)]
    all_to_all x0 -> x2, blocking collectives: none -> 33.7 us  [the longest x1 18 us: per_device(): walked = lax.all_to_all(walked, AXES, 0, 0, tiled=True)]
  transfers between devices with their start and end apart: 22 -> 4, of which waited for: 21 -> 3; matrix products, arithmetic and copies ran while one was open for 5% -> 3% of each run, Pallas kernels for 0% -> 4%
where the time goes in v1:
time: 583 us; the launch traced here: 571 us
  waiting for transfers between devices  173 us (30%)
  matrix products  146 us (25%)
  local copies, waits for them, and re-layouts  75.9 us (13%)
  blocking collectives  75.3 us (13%)
  Pallas kernels  54.2 us (9%)
  other arithmetic  24.4 us (4%)
  between operations  16 us (3%)
  starting transfers between devices  6.43 us (1%)
    psum x1, waiting for transfers between devices, per_device(): lax.psum((grad_w_input, grad_bias_input, grad_gain_attn, grad_shift_attn,...  87.9 us
    all_gather x1, waiting for transfers between devices, per_device(): everything = lax.all_gather(values, AXES, axis=0, tiled=True)  64.7 us
    pallas_call x2, Pallas kernels, walk(): pl.pallas_call(functools.partial(walk_kernel, forward, HOPS, slots, n_col...  54.2 us
    psum x1, blocking collectives, per_device(): lax.psum((grad_w_input, grad_bias_input, grad_gain_attn, grad_shift_attn,...  41.5 us
    dot_general x3, matrix products, node_tail(): projected = jnp.einsum('ntd,de->nte', normed, w_heads, precision=near)  32.4 us
    dot_general x3, matrix products, node_tail(): jnp.einsum('nhqk,nkhe->nqhe', attention, value_rows, precision=near)  27.7 us
    dot_general x3, matrix products, node_tail(): jnp.einsum('nqhe,nkhe->nhqk', queries, key_rows, precision=near)  26.6 us
    all_to_all x1, waiting for transfers between devices, per_device(): back = lax.all_to_all(sent, AXES, 0, 0, tiled=True)  19.5 us
  transfers between devices with their start and end apart: 4, of which 3 were waited for; matrix products, arithmetic and copies ran while one was open for 3% of the time, Pallas kernels for 4%

profile of v1, /device:TPU:0, one launch (start us, length us, event | category | flops | bytes accessed | tf_op | source)
XLA Modules:
  0.0 571.4 jit_solution(16101674322376633779)
XLA Ops:
  10.5 15.7 %all_to_all.20.field_ref = f32[32,8,128]{2,1,0:T(8,128)S(1)} all-to-all(f32[32,8,128]{2,1,0:T(8,128)S(1)} %pad_maximum_fusion), channel_id=1, replica_groups=mesh['row'=16,'col'=2] {'row','col'}, dimensions={0} | all-to-all | bytes 262144 | tf_op jit(solution)/shard_map/all_to_all | solution.py:245
  26.3 64.7 %all-gather.3.cloned.1.call-done = f32[1,1,128,128,128]{4,3,1,0,2:T(8,128)} async-done(((f32[1,1,4,128,128]{4,3,1,0,2:T(8,128)}), f32[1,1,128,128,128]{4,3,1,0,2:T(8,128)}) %all-gather.3.cloned.1.call-update) | async-done | bytes 8388624 | tf_op jit(solution)/shard_map/all_gather | solution.py:235
  91.0 29.9 %walk_forward.1 = f32[32,32,128]{2,1,0:T(8,128)S(1)} custom-call(s32[32,9]{1,0:T(8,128)S(1)} %convert_bitcast_fusion.meta_ref, f32[32,8,128]{2,1,0:T(8,128)S(1)} %all_to_all.20.field_ref, f32[128,128,128]{2,1,0:T(8,128)} %bitcast.147), custom_call_target="tpu_custom_call" | custom-call | tf_op jit(solution)/shard_map/walk_forward/pallas_call | solution.py:119
  121.0 18.0 %all_to_all.21 = f32[32,32,128]{2,1,0:T(8,128)S(1)} all-to-all(f32[32,32,128]{2,1,0:T(8,128)S(1)} %walk_forward.1), channel_id=1, replica_groups=mesh['row'=16,'col'=2] {'row','col'}, dimensions={0} | all-to-all | bytes 1048576 | tf_op jit(solution)/shard_map/all_to_all | solution.py:248
  142.4 5.5 fusion.10
  153.7 5.6 copy.95
  162.2 5.6 copy.94
  170.6 5.8 %copy.96 = f32[128,8,8,64]{3,1,2,0:T(8,128)} copy(f32[128,8,8,64]{0,3,2,1:T(8,128)} %bitcast.153) | data formatting | bytes 4194304 | tf_op jit(solution)/shard_map/jvp()/reshape | solution.py:171
  176.4 7.4 %multiply_reduce_fusion.1 = (f32[128,8,8]{2,1,0:T(8,128)S(1)}, f32[128,8,8,8]{2,3,1,0:T(8,128)S(1)}) fusion(f32[128,8,8,64]{3,1,2,0:T(8,128)} %copy.94, f32[128,8,8,64]{3,1,2,0:T(8,128)} %copy.95), kind=kOutput, calls=%fused_computation.27 | convolution fusion | flops 25288704 | bytes 4489216 | tf_op jit(solution)/shard_map/jvp(nqhe,nkhe->nhqk)/dot_general | solution.py:172
  188.0 5.9 %convolution_bitcast_fusion.3 = f32[128,8,8,64]{3,1,2,0:T(8,128)} fusion(f32[128,8,8,64]{3,1,2,0:T(8,128)S(1)} %copy-done.17, f32[128,8,8]{2,1,0:T(8,128)S(1)} %fusion.59, f32[128,8,8,8]{2,3,1,0:T(8,128)S(1)} %get-tuple-element.113, f32[128,8,8]{2,1,0:T(8,128)S(1)} %get-tuple-element.112), kind=kOutput, calls=%fused_computation.37 | convolution fusion | flops 25362432 | bytes 4521984 | tf_op jit(solution)/shard_map/jvp(nhqk,nkhe->nqhe)/dot_general | solution.py:174
  194.0 5.0 copy.98
  199.0 4.8 fusion.86
  204.3 4.9 fusion.47
  209.2 9.5 %fusion.2 = f32[128,8,1024]{2,0,1:T(8,128)S(1)} fusion(f32[128,8,1024]{2,0,1:T(8,128)S(1)} %get-tuple-element.116, f32[1024]{0:T(1024)S(1)} %copy-done.41, u8[128,1024]{1,0:T(8,128)(4,1)S(1)} %get-tuple-element.81, u8[128,1024]{1,0:T(8,128)(4,1)S(1)} %get-tuple-element.80), kind=kLoop, calls=%fused_computation.4 | loop fusion | flops 71303168 | bytes 8654848 | tf_op jit(solution)/shard_map/jvp()/erfc | solution.py:179
  231.9 7.7 %convolution_bitcast_fusion.4 = f32[1024,512]{1,0:T(8,128)} fusion(f32[128,8,1024]{2,0,1:T(8,128)} %copy-done.9, f32[128,8,1024]{2,0,1:T(8,128)} %copy-done.7, f32[1024]{0:T(1024)S(1)} %copy-done.41, f32[128,1,512]{2,0,1:T(8,128)S(1)} %bitcast.158, f32[128,7,512]{2,0,1:T(8,128)S(1)} %multiply_add_fusion.3), kind=kOutput, calls=%fused_computation.67 | convolution fusion | flops 3224895488 | bytes 12587008 | tf_op jit(solution)/shard_map/transpose(jvp(nte,ed->ntd))/dot_general | solution.py:183
  239.7 5.8 %fusion.87 = (f32[1024]{0:T(1024)}, f32[128,8,1024]{2,0,1:T(8,128)S(1)}) fusion(f32[128,8,1024]{2,0,1:T(8,128)S(1)} %copy-done.10, f32[1024,512]{1,0:T(8,128)S(1)} %copy-done.33, f32[128,1,512]{2,0,1:T(8,128)S(1)} %bitcast.159, f32[128,7,512]{2,0,1:T(8,128)S(1)} %multiply_add_fusion.3, f32[128,8,1024]{2,0,1:T(8,128)S(1)} %copy-done.8, f32[1024]{0:T(1024)S(1)} %copy-done.41), kind=kOutput, calls=%fused_computation.150 | convolution fusion | flops 3237477376 | bytes 16785408 | tf_op jit(solution)/shard_map/transpose(jvp(nte,ed->ntd))/dot_general | solution.py:183
  245.5 5.2 fusion.24
  250.7 4.7 fusion.81
  264.8 5.6 copy.101
  270.4 12.5 %multiply_reduce_fusion = (f32[128,8,8]{2,1,0:T(8,128)}, f32[128,8,8,8]{2,3,1,0:T(8,128)}) fusion(f32[128,8,8]{2,1,0:T(8,128)} %multiply_divide_fusion, f32[128,8,8]{2,1,0:T(8,128)} %copy-done.18, f32[128,8,8,8]{2,3,1,0:T(8,128)} %copy-done.5, f32[128,8,64,8]{2,3,1,0:T(8,128)} %copy.101, f32[128,8,8,64]{3,1,2,0:T(8,128)} %copy.96), kind=kOutput, calls=%fused_computation.11 | convolution fusion | flops 25485312 | bytes 4816896 | tf_op jit(solution)/shard_map/transpose(jvp(nhqk,nkhe->nqhe))/dot_general | solution.py:174
  284.7 8.2 %convolution_bitcast_fusion = f32[128,8,8,64]{3,1,2,0:T(8,128)} fusion(f32[128,8,8,64]{3,1,2,0:T(8,128)S(1)} %copy-done.16, f32[128,8,8,8]{2,3,1,0:T(8,128)} %get-tuple-element.119, f32[128,8,8]{2,1,0:T(8,128)S(1)} %neg.29, f32[128,8,8]{2,1,0:T(8,128)S(1)} %copy-done.29, f32[128,8,8]{2,1,0:T(8,128)S(1)} %copy-done.19, f32[128,8,8,8]{2,3,1,0:T(8,128)S(1)} %copy-done.6), kind=kOutput, calls=%fused_computation.34 | convolution fusion | flops 25559040 | bytes 4816896 | tf_op jit(solution)/shard_map/transpose(jvp(nqhe,nkhe->nhqk))/dot_general | solution.py:172
  293.0 10.9 %convolution_bitcast_fusion.1 = f32[128,8,8,64]{3,1,2,0:T(8,128)} fusion(f32[128,8,8,64]{3,1,2,0:T(8,128)} %copy.94, f32[128,8,8,8]{2,3,1,0:T(8,128)} %get-tuple-element.119, f32[128,8,8]{2,1,0:T(8,128)} %copy-done.39, f32[128,8,8]{2,1,0:T(8,128)S(1)} %copy-done.29, f32[128,8,8]{2,1,0:T(8,128)S(1)} %copy-done.19, f32[128,8,8,8]{2,3,1,0:T(8,128)} %copy-done.5), kind=kOutput, calls=%fused_computation.35 | convolution fusion | flops 25559040 | bytes 4816896 | tf_op jit(solution)/shard_map/transpose(jvp(nqhe,nkhe->nhqk))/dot_general | solution.py:172
  303.9 9.4 %convolution_bitcast_fusion.2 = f32[128,8,8,64]{3,1,2,0:T(8,128)} fusion(f32[128,8,64,8]{2,3,1,0:T(8,128)} %copy.101, f32[128,8,8]{2,1,0:T(8,128)S(1)} %copy-done.29, f32[128,8,8,8]{2,3,1,0:T(8,128)} %copy-done.5, f32[128,8,8]{2,1,0:T(8,128)S(1)} %copy-done.19), kind=kOutput, calls=%fused_computation.36 | convolution fusion | flops 25362432 | bytes 4521984 | tf_op jit(solution)/shard_map/transpose(jvp(nhqk,nkhe->nqhe))/dot_general | solution.py:174
  313.3 4.9 copy.102
  318.2 4.8 copy.106
  322.9 4.8 copy.109
  327.7 14.6 %fusion.82 = (f32[512]{0:T(512)}, f32[128,8]{0,1:T(8,128)S(1)}, f32[128,8,512]{2,0,1:T(8,128)S(1)}) fusion(f32[512]{0:T(512)S(1)} %copy-done.44, f32[128,8]{0,1:T(8,128)S(1)} %broadcast_multiply_fusion.1, f32[128,8,512]{2,0,1:T(8,128)} %copy-done.3, f32[512]{0:T(512)S(1)} %copy-done.40, f32[512,1536]{1,0:T(8,128)S(1)} %copy-done, ...), kind=kOutput, calls=%fused_computation.145 | convolution fusion | flops 4838128128 | bytes 13645824 | tf_op jit(solution)/shard_map/transpose(jvp(ntd,de->nte))/dot_general | solution.py:166
  342.4 12.2 %fusion.8 = f32[512,1536]{1,0:T(8,128)} fusion(f32[128,8,512]{0,2,1:T(8,128)S(1)} %bitcast.167, f32[128,8,512]{0,2,1:T(8,128)S(1)} %bitcast.165, f32[128,8,512]{0,2,1:T(8,128)S(1)} %bitcast.163, f32[512]{0:T(512)S(1)} %copy-done.51, f32[512]{0:T(512)S(1)} %copy-done.44, f32[128,8]{0,1:T(8,128)S(1)} %fusion.66, f32[128,8,512]{2,0,1:T(8,128)S(1)} %copy-done.4, ...), kind=kOutput, calls=%fused_computation.28 | convolution fusion | flops 4837605376 | bytes 11548672 | tf_op jit(solution)/shard_map/transpose(jvp(ntd,de->nte))/dot_general | solution.py:166
  373.7 19.5 %all-to-all-done.2.field_ref = f32[32,32,128]{2,1,0:T(8,128)} async-done(((f32[32,32,128]{2,1,0:T(8,128)}), f32[32,32,128]{2,1,0:T(8,128)}, u32[]{:S(2)}, u32[]{:S(2)}) %all-to-all-start.2) | async-done | bytes 524320 | tf_op jit(solution)/shard_map/all_to_all | solution.py:341
  393.2 24.3 %walk_backward.1 = f32[32,8,128]{2,1,0:T(8,128)} custom-call(s32[32,9]{1,0:T(8,128)S(1)} %convert_bitcast_fusion.meta_ref, f32[32,32,128]{2,1,0:T(8,128)} %all-to-all-done.2.field_ref, f32[128,128,128]{2,1,0:T(8,128)} %bitcast.148), custom_call_target="tpu_custom_call" | custom-call | tf_op jit(solution)/shard_map/walk_backward/pallas_call | solution.py:119
  422.1 41.5 %all-reduce.6 = (f32[512]{0:T(512)}, f32[512]{0:T(512)}, f32[512]{0:T(512)}, f32[512]{0:T(512)}, f32[512]{0:T(512)}, /*index=5*/f32[512]{0:T(512)}, f32[1024]{0:T(1024)}, f32[512]{0:T(512)}, f32[512]{0:T(512)}) all-reduce(f32[512]{0:T(512)} %get-tuple-element.102, ...), channel_id=1, replica_groups=mesh['row'=16,'col'=2] {'row','col'}, use_global_device_ids=true, to_apply=%region_16.0 | all-reduce | flops 5120 | bytes 40960 | tf_op jit(solution)/shard_map/psum | solution.py:360
  466.9 87.9 %all-reduce.10.cloned.1.call-done = (f32[128,512]{1,0:T(8,128)}, f32[512,1536]{1,0:T(8,128)}, f32[512,512]{1,0:T(8,128)}, f32[512,1024]{1,0:T(8,128)}, f32[1024,512]{1,0:T(8,128)}) async-done(((f32[128,512]{1,0:T(8,128)}, f32[512,1536]{1,0:T(8,128)}, f32[512,512]{1,0:T(8,128)}, f32[512,1024]{1,0:T(8,128)}, f32[1024,512]{1,0:T(8,128)}), (f32[128,512]{1,0:T(8,128)}, f32[512,1536]{1,0:T(8,128)}, ...) | async-done | bytes 8650768 | tf_op jit(solution)/shard_map/psum | solution.py:360
  (171 shorter events, 82.8 us)
Async XLA Ops:
  7.2 135.2 %copy-start = (f32[512,1536]{1,0:T(8,128)S(1)}, f32[512,1536]{1,0:T(8,128)}, u32[]{:S(2)}) copy-start(f32[512,1536]{1,0:T(8,128)} %param.31) | copy-start | bytes 9437188
  7.2 83.8 %all-gather.3.cloned.1.call-start = ((), (), s32[]{:S(2)}) async-start(), calls=%async_computation.4 | async-start | bytes 8650752 | tf_op jit(solution)/shard_map/all_gather | solution.py:235
  7.9 546.9 %all-reduce.10.cloned.1.call-start = ((), (), s32[]{:S(2)}) async-start(), calls=%async_computation.5 | async-start | bytes 17301504 | tf_op jit(solution)/shard_map/psum | solution.py:360
  91.0 48.8 %copy-start.37 = (f32[128,512]{1,0:T(8,128)S(1)}, f32[128,512]{1,0:T(8,128)}, u32[]{:S(2)}) copy-start(f32[128,512]{1,0:T(8,128)} %param.27) | copy-start | bytes 786436
  91.0 48.8 %copy-start.40 = (f32[512]{0:T(512)S(1)}, f32[512]{0:T(512)}, u32[]{:S(2)}) copy-start(f32[512]{0:T(512)} %param.28) | copy-start | bytes 6148
  121.0 21.4 %copy-start.44 = (f32[512]{0:T(512)S(1)}, f32[512]{0:T(512)}, u32[]{:S(2)}) copy-start(f32[512]{0:T(512)} %param.29) | copy-start | bytes 6148
  121.0 21.4 %copy-start.50 = (f32[512]{0:T(512)S(1)}, f32[512]{0:T(512)}, u32[]{:S(2)}) copy-start(f32[512]{0:T(512)} %param.30) | copy-start | bytes 6148
  198.9 5.3 copy-start.34
  203.8 14.9 %copy-start.1 = (f32[128,8,512]{2,0,1:T(8,128)}, f32[128,8,512]{2,0,1:T(8,128)S(1)}, u32[]{:S(2)}) copy-start(f32[128,8,512]{2,0,1:T(8,128)S(1)} %get-tuple-element.115) | copy-start | bytes 6291460
  209.1 9.5 %copy-start.7 = (f32[128,8,1024]{2,0,1:T(8,128)}, f32[128,8,1024]{2,0,1:T(8,128)S(1)}, u32[]{:S(2)}) copy-start(f32[128,8,1024]{2,0,1:T(8,128)S(1)} %get-tuple-element.116) | copy-start | bytes 12582916
  209.2 9.5 %copy-start.32 = (f32[1024,512]{1,0:T(8,128)S(1)}, f32[1024,512]{1,0:T(8,128)}, u32[]{:S(2)}) copy-start(f32[1024,512]{1,0:T(8,128)} %param.38) | copy-start | bytes 6291460
  209.2 9.5 %copy-start.47 = (f32[512]{0:T(512)S(1)}, f32[512]{0:T(512)}, u32[]{:S(2)}) copy-start(f32[512]{0:T(512)} %param.39) | copy-start | bytes 6148
  218.7 5.6 copy-start.45
  231.6 8.1 %copy-start.42 = (f32[128,7]{0,1:T(8,128)}, f32[128,7]{0,1:T(8,128)S(1)}, u32[]{:S(2)}) copy-start(f32[128,7]{0,1:T(8,128)S(1)} %get-tuple-element.108) | copy-start | bytes 10756
  231.9 7.8 %copy-start.8 = (f32[128,8,1024]{2,0,1:T(8,128)S(1)}, f32[128,8,1024]{2,0,1:T(8,128)}, u32[]{:S(2)}) copy-start(f32[128,8,1024]{2,0,1:T(8,128)} %copy-done.7) | copy-start | bytes 12582916
  231.9 7.8 %copy-start.10 = (f32[128,8,1024]{2,0,1:T(8,128)S(1)}, f32[128,8,1024]{2,0,1:T(8,128)}, u32[]{:S(2)}) copy-start(f32[128,8,1024]{2,0,1:T(8,128)} %copy-done.9) | copy-start | bytes 12582916
  231.9 7.8 %copy-start.33 = (f32[1024,512]{1,0:T(8,128)S(1)}, f32[1024,512]{1,0:T(8,128)}, u32[]{:S(2)}) copy-start(f32[1024,512]{1,0:T(8,128)} %param.38) | copy-start | bytes 6291460
  239.7 5.8 %copy-start.2 = (f32[128,8,512]{2,0,1:T(8,128)S(1)}, f32[128,8,512]{2,0,1:T(8,128)}, u32[]{:S(2)}) copy-start(f32[128,8,512]{2,0,1:T(8,128)} %copy-done.1) | copy-start | bytes 6291460
  239.7 5.8 %copy-start.49 = (f32[512]{0:T(512)S(1)}, f32[512]{0:T(512)}, u32[]{:S(2)}) copy-start(f32[512]{0:T(512)} %param.35) | copy-start | bytes 6148
  258.6 6.2 %copy-start.11 = (f32[128,8,512]{2,0,1:T(8,128)}, f32[128,8,512]{2,0,1:T(8,128)S(1)}, u32[]{:S(2)}) copy-start(f32[128,8,512]{2,0,1:T(8,128)S(1)} %get-tuple-element.101) | copy-start | bytes 6291460
  270.4 14.3 %copy-start.6 = (f32[128,8,8,8]{2,3,1,0:T(8,128)S(1)}, f32[128,8,8,8]{2,3,1,0:T(8,128)}, u32[]{:S(2)}) copy-start(f32[128,8,8,8]{2,3,1,0:T(8,128)} %copy-done.5) | copy-start | bytes 786436
  270.4 14.3 %copy-start.16 = (f32[128,8,8,64]{3,1,2,0:T(8,128)S(1)}, f32[128,8,8,64]{3,1,2,0:T(8,128)}, u32[]{:S(2)}) copy-start(f32[128,8,8,64]{3,1,2,0:T(8,128)} %copy.95) | copy-start | bytes 6291460
  270.4 14.3 %copy-start.19 = (f32[128,8,8]{2,1,0:T(8,128)S(1)}, f32[128,8,8]{2,1,0:T(8,128)}, u32[]{:S(2)}) copy-start(f32[128,8,8]{2,1,0:T(8,128)} %copy-done.18) | copy-start | bytes 98308
  270.4 14.3 %copy-start.29 = (f32[128,8,8]{2,1,0:T(8,128)S(1)}, f32[128,8,8]{2,1,0:T(8,128)}, u32[]{:S(2)}) copy-start(f32[128,8,8]{2,1,0:T(8,128)} %copy-done.28) | copy-start | bytes 98308
  327.7 14.6 %copy-start.4 = (f32[128,8,512]{2,0,1:T(8,128)S(1)}, f32[128,8,512]{2,0,1:T(8,128)}, u32[]{:S(2)}) copy-start(f32[128,8,512]{2,0,1:T(8,128)} %copy-done.3) | copy-start | bytes 6291460
  327.7 14.6 %copy-start.25 = (f32[128,8,8,64]{0,3,2,1:T(8,128)S(1)}, f32[128,8,8,64]{0,3,2,1:T(8,128)}, u32[]{:S(2)}) copy-start(f32[128,8,8,64]{0,3,2,1:T(8,128)} %copy.102) | copy-start | bytes 6291460
  327.7 14.6 %copy-start.26 = (f32[128,8,8,64]{0,3,2,1:T(8,128)S(1)}, f32[128,8,8,64]{0,3,2,1:T(8,128)}, u32[]{:S(2)}) copy-start(f32[128,8,8,64]{0,3,2,1:T(8,128)} %copy.106) | copy-start | bytes 6291460
  327.7 14.6 %copy-start.27 = (f32[128,8,8,64]{0,3,2,1:T(8,128)S(1)}, f32[128,8,8,64]{0,3,2,1:T(8,128)}, u32[]{:S(2)}) copy-start(f32[128,8,8,64]{0,3,2,1:T(8,128)} %copy.109) | copy-start | bytes 6291460
  327.7 14.6 %copy-start.51 = (f32[512]{0:T(512)S(1)}, f32[512]{0:T(512)}, u32[]{:S(2)}) copy-start(f32[512]{0:T(512)} %param.30) | copy-start | bytes 6148
  366.2 27.0 %all-to-all-start.2 = ((f32[32,32,128]{2,1,0:T(8,128)}), f32[32,32,128]{2,1,0:T(8,128)}, u32[]{:S(2)}, u32[]{:S(2)}) async-start(f32[32,32,128]{2,1,0:T(8,128)} %bitcast.168), calls=%async_computation.2 | async-start | bytes 1048576 | tf_op jit(solution)/shard_map/all_to_all | solution.py:341
  417.5 47.9 %all-to-all-start.3 = ((f32[32,8,128]{2,1,0:T(8,128)}), f32[32,8,128]{2,1,0:T(8,128)S(1)}, u32[]{:S(2)}, u32[]{:S(2)}) async-start(f32[32,8,128]{2,1,0:T(8,128)} %walk_backward.1), calls=%async_computation.3 | async-start | bytes 262144 | tf_op jit(solution)/shard_map/all_to_all | solution.py:343
  554.9 5.7 copy-start.36
  (24 other events, 69.6 us)
Sparse Core Ops, SparseCore 0:
  11.0 79.9 all-gather.2
  360.9 193.8 all-reduce.9

commit v2 on v1

v2 whole, which is shorter than its diff:
```python
import functools
import math

import jax
import jax.numpy as jnp
from jax import lax
from jax.experimental import pallas as pl
from jax.experimental.pallas import tpu as pltpu
from jax.sharding import PartitionSpec as P

HEADS = 8
HEAD_DIM = 64
HOPS = 7
TOKENS = HOPS + 1


exact = lax.Precision.HIGHEST
AXES = ("row", "col")
LANES = 128
PIECE = 4
UNROLL = 16
NODES_STEP = 32


def block_list(meta_ref, source, taken, given, slots, n_col, row_blocks):
    def tile(position, live):
        row, col = position // n_col, position % n_col
        count = meta_ref[position, 2 * slots]
        for slot in range(slots):
            source[live] = position * slots + slot
            given[live] = row * row_blocks + meta_ref[position, slot]
            taken[live] = meta_ref[position, slots + slot] * n_col + col
            live = live + jnp.where(slot < count, 1, 0)
        return live

    tiles = meta_ref.shape[0]
    live = lax.fori_loop(0, tiles, tile, jnp.int32(0))
    for extra in range(UNROLL):
        source[live + extra] = 0
        given[live + extra] = tiles
        taken[live + extra] = tiles
    return (live + UNROLL - 1) // UNROLL


def walk_kernel(
    forward, hops, slots, n_col, row_blocks, meta_ref, field_ref, values_ref, out_ref, pairs, total, state, source, taken, given
):
    if forward:
        steps = block_list(meta_ref, source, taken, given, slots, n_col, row_blocks)
    else:
        steps = block_list(meta_ref, source, given, taken, slots, n_col, row_blocks)
    blocks = field_ref.shape[0]

    def split_some(step, _):
        for inner in range(4):
            place = step * 4 + inner
            block = values_ref[source[place]]
            upper, lower = split(block.T if forward else block)
            pairs[place, :LANES] = upper
            pairs[place, LANES:] = lower
        return 0

    lax.fori_loop(0, steps * (UNROLL // 4), split_some, 0)
    state[blocks] = jnp.zeros_like(state[blocks])
    is_top = lax.broadcasted_iota(jnp.int32, (blocks, 2 * PIECE, LANES), 1) < PIECE

    def keep(field):
        doubled = jnp.concatenate([field, field], axis=1)
        rounded = doubled.astype(jnp.bfloat16).astype(jnp.float32)
        state[:blocks] = jnp.where(is_top, rounded, doubled - rounded)

    def apply():
        total[...] = jnp.zeros_like(total)

        def some(step, _):
            products = []
            for inner in range(UNROLL):
                place = step * UNROLL + inner
                rows = state[taken[place]].astype(jnp.bfloat16)
                rows = jnp.concatenate([rows, rows], axis=1)
                products.append(dot(rows, pairs[place], 1, 0))
            for inner in range(UNROLL):
                target = given[step * UNROLL + inner]
                total[target] = total[target] + products[inner]
            return 0

        lax.fori_loop(0, steps, some, 0)
        summed = total[:blocks]
        return summed[:, :PIECE] + summed[:, PIECE:]

    if forward:
        field = field_ref[:, :PIECE]
        out_ref[:, :PIECE] = field
        keep(field)
        for hop in range(1, hops + 1):
            field = apply()
            out_ref[:, hop * PIECE : (hop + 1) * PIECE] = field
            if hop < hops:
                keep(field)
    else:
        field = field_ref[:, hops * PIECE :]
        for hop in range(hops - 1, -1, -1):
            keep(field)
            field = apply()
            if hop > 0:
                field = field + field_ref[:, hop * PIECE : (hop + 1) * PIECE]
        out_ref[:, :PIECE] = field
        out_ref[:, PIECE:] = field


def walk(forward, meta, field, values, n_col, row_blocks):
    blocks = field.shape[0]
    slots = values.shape[0] // meta.shape[0]
    room = values.shape[0] + UNROLL
    out_rows = (HOPS + 1) * PIECE if forward else 2 * PIECE
    return pl.pallas_call(
        functools.partial(walk_kernel, forward, HOPS, slots, n_col, row_blocks),
        out_shape=jax.ShapeDtypeStruct((blocks, out_rows, LANES), jnp.float32),
        in_specs=[
            pl.BlockSpec(memory_space=pltpu.SMEM),
            pl.BlockSpec(memory_space=pltpu.VMEM),
            pl.BlockSpec(memory_space=pltpu.VMEM),
        ],
        out_specs=pl.BlockSpec(memory_space=pltpu.VMEM),
        scratch_shapes=[
            pltpu.VMEM((room, 2 * LANES, LANES), jnp.bfloat16),
            pltpu.VMEM((blocks + 1, 2 * PIECE, LANES), jnp.float32),
            pltpu.VMEM((blocks + 1, 2 * PIECE, LANES), jnp.float32),
            pltpu.SMEM((room,), jnp.int32),
            pltpu.SMEM((room,), jnp.int32),
            pltpu.SMEM((room,), jnp.int32),
        ],
        compiler_params=pltpu.CompilerParams(vmem_limit_bytes=48 << 20),
        cost_estimate=work(20),
        name="walk_forward" if forward else "walk_backward",
    )(meta, field, values)


def work(microseconds):
    return pl.CostEstimate(
        flops=microseconds * 1_000_000_000,
        bytes_accessed=microseconds * 3_000_000,
        transcendentals=0,
    )


def split(values):
    upper = values.astype(jnp.bfloat16)
    return upper, (values - upper.astype(jnp.float32)).astype(jnp.bfloat16)


def dot(left, right, left_axis, right_axis):
    return lax.dot_general(
        left, right, (((left_axis,), (right_axis,)), ((), ())), preferred_element_type=jnp.float32
    )


def product(left, right, left_axis, right_axis):
    return dot(
        jnp.concatenate([left[0], left[0], left[1]], axis=left_axis),
        jnp.concatenate([right[0], right[1], right[0]], axis=right_axis),
        left_axis,
        right_axis,
    )


def pair(upper_ref, lower_ref):
    return upper_ref[...], lower_ref[...]


def standard(values):
    centred = values - jnp.mean(values, axis=-1, keepdims=True)
    scale = lax.rsqrt(jnp.mean(centred * centred, axis=-1, keepdims=True) + 1e-05)
    return centred * scale, scale


def standard_back(upstream, normed, scale):
    average = jnp.mean(upstream, axis=-1, keepdims=True)
    along = jnp.mean(upstream * normed, axis=-1, keepdims=True)
    return (upstream - average - normed * along) * scale


def column_sum(values):
    return jnp.sum(values, axis=0, keepdims=True)


def head_tables(columns):
    row = lax.broadcasted_iota(jnp.int32, (columns, LANES), 0) // HEAD_DIM
    lane = lax.broadcasted_iota(jnp.int32, (columns, LANES), 1) % HEADS
    gather = jnp.where(row == lane, 1.0, 0.0).astype(jnp.bfloat16)
    row = lax.broadcasted_iota(jnp.int32, (LANES, columns), 0) % HEADS
    lane = lax.broadcasted_iota(jnp.int32, (LANES, columns), 1) // HEAD_DIM
    spread = jnp.where(row == lane, 1.0, 0.0).astype(jnp.bfloat16)
    return gather, spread


def per_head(values, gather):
    upper, lower = split(values)
    return dot(
        jnp.concatenate([upper, lower], axis=1), jnp.concatenate([gather, gather], axis=0), 1, 0
    )


def over_columns(values, spread):
    upper, lower = split(values)
    return dot(
        jnp.concatenate([upper, lower], axis=1), jnp.concatenate([spread, spread], axis=0), 1, 0
    )


def lane_group(rows):
    return lax.broadcasted_iota(jnp.int32, (rows, LANES), 1) // HEADS


def token_scores(left, right, gather, nodes, columns):
    group = lane_group(nodes)
    kept = [jnp.zeros((nodes, LANES), jnp.float32) for _ in range(TOKENS // 2)]
    for key in range(TOKENS):
        sums = per_head((left() * right(key)[None]).reshape(TOKENS * nodes, columns), gather)
        for query in range(TOKENS):
            part = sums[query * nodes : (query + 1) * nodes]
            kept[query // 2] = jnp.where(group == 2 * key + query % 2, part, kept[query // 2])
    return jnp.concatenate(kept, axis=0)


def over_keys(values, combine):
    for shift in (2 * HEADS, 4 * HEADS, 8 * HEADS):
        values = combine(values, pltpu.roll(values, shift, 1))
    return values


def one_key(table, key, spread, nodes):
    group = lane_group(nodes)
    rows = [
        jnp.where(
            group == 2 * key + query % 2,
            table[(query // 2) * nodes : (query // 2 + 1) * nodes],
            0.0,
        )
        for query in range(TOKENS)
    ]
    return over_columns(jnp.concatenate(rows, axis=0), spread)


def front_kernel(
    hops_ref,
    cotangent_ref,
    wi_h,
    wi_l,
    wh_h,
    wh_l,
    wm_h,
    wm_l,
    we_h,
    we_l,
    wr_h,
    wr_l,
    bias_input,
    gain_attn,
    shift_attn,
    bias_merge,
    gain_ffn,
    shift_ffn,
    bias_expand,
    bias_reduce,
    readout,
    out_ref,
    z0_ref,
    heads_ref,
    probs_ref,
    mixed_ref,
    dz1_ref,
    first,
    second,
    small,
    u_h,
    u_l,
    a_h,
    a_l,
    d_h,
    d_l,
    slope,
    z1_ref,
    n2_ref,
):
    nodes = hops_ref.shape[1]
    rows = TOKENS * nodes
    columns = z0_ref.shape[2]

    @pl.when(pl.program_id(0) == 0)
    def _():
        first[...] = jnp.zeros_like(first)
        second[...] = jnp.zeros_like(second)
        small[...] = jnp.zeros_like(small)

    def by_token(values):
        return values.reshape(TOKENS, nodes, values.shape[-1])

    hops = split(hops_ref[...].reshape(rows, hops_ref.shape[2]))
    z0 = product(hops, pair(wi_h, wi_l), 1, 0) + bias_input[...]
    z0_ref[...] = by_token(z0)
    n1, _ = standard(z0)
    u_h[...], u_l[...] = split(n1 * gain_attn[...] + shift_attn[...])
    heads_ref[...] = by_token(product(pair(u_h, u_l), pair(wh_h, wh_l), 1, 0))
    gather, spread = head_tables(columns)
    scores = token_scores(
        lambda: heads_ref[:, :, :columns],
        lambda key: heads_ref[key, :, columns : 2 * columns],
        gather,
        nodes,
        columns,
    ) * (1.0 / math.sqrt(HEAD_DIM))
    raised = jnp.exp(scores - over_keys(scores, jnp.maximum))
    probs = raised / over_keys(raised, jnp.add)
    probs_ref[...] = probs.reshape(TOKENS // 2, nodes, LANES)
    for key in range(TOKENS):
        term = by_token(one_key(probs, key, spread, nodes)) * heads_ref[key, :, 2 * columns :][None]
        mixed_ref[...] = term if key == 0 else mixed_ref[...] + term
    u_h[...], u_l[...] = split(mixed_ref[...].reshape(rows, columns))
    z1 = (
        z0_ref[...].reshape(rows, columns)
        + product(pair(u_h, u_l), pair(wm_h, wm_l), 1, 0)
        + bias_merge[...]
    )
    z1_ref[...] = z1
    n2, scale = standard(z1)
    n2_ref[...] = n2
    u_h[...], u_l[...] = split(n2 * gain_ffn[...] + shift_ffn[...])
    pre = product(pair(u_h, u_l), pair(we_h, we_l), 1, 0) + bias_expand[...]
    below = 0.5 * (1.0 + lax.erf(pre * math.sqrt(0.5)))
    slope[...] = below + pre * jnp.exp(-0.5 * pre * pre) * (1.0 / math.sqrt(2.0 * math.pi))
    a_h[...], a_l[...] = split(pre * below)
    z2 = by_token(
        z1_ref[...] + product(pair(a_h, a_l), pair(wr_h, wr_l), 1, 0) + bias_reduce[...]
    )
    marks = jnp.sum(z2[1:] * readout[...][None], axis=-1, keepdims=True)
    raised = jnp.exp(marks - jnp.max(marks, axis=0, keepdims=True))
    alpha = raised / jnp.sum(raised, axis=0, keepdims=True)
    out_ref[...] = z2[0] + jnp.sum(alpha * z2[1:], axis=0)
    cotangent = cotangent_ref[...]
    along = jnp.sum(cotangent[None] * z2[1:], axis=-1, keepdims=True)
    slant = alpha * (along - jnp.sum(alpha * along, axis=0, keepdims=True))
    small[0:1] += column_sum(jnp.sum(slant * z2[1:], axis=0))
    dz2 = jnp.concatenate(
        [cotangent[None], alpha * cotangent[None] + slant * readout[...][None]], axis=0
    ).reshape(rows, columns)
    dz1_ref[...] = by_token(dz2)
    d_h[:, :columns], d_l[:, :columns] = split(dz2)
    small[1:2] += column_sum(dz2)
    near = (d_h[:, :columns], d_l[:, :columns])
    wide = a_h.shape[1]
    first[:wide] += product(pair(a_h, a_l), near, 0, 0)
    dpre = product(near, pair(wr_h, wr_l), 1, 1) * slope[...]
    total = column_sum(dpre)
    small[2:3] += total[:, :columns]
    small[5:6] += total[:, columns:]
    d_h[...], d_l[...] = split(dpre)
    grown = product(pair(u_h, u_l), pair(d_h, d_l), 0, 0)
    second[:columns] += grown[:, :columns]
    second[columns : 2 * columns] += grown[:, columns:]
    du2 = product(pair(d_h, d_l), pair(we_h, we_l), 1, 1)
    n2 = n2_ref[...]
    small[3:4] += column_sum(du2 * n2)
    small[4:5] += column_sum(du2)
    dz1 = dz1_ref[...].reshape(rows, columns) + standard_back(du2 * gain_ffn[...], n2, scale)
    dz1_ref[...] = by_token(dz1)
    d_h[:, :columns], d_l[:, :columns] = split(dz1)
    u_h[...], u_l[...] = split(mixed_ref[...].reshape(rows, columns))
    grown = product(pair(u_h, u_l), (d_h[:, :columns], d_l[:, :columns]), 0, 0)
    first[wide:] += grown[: columns // 2]
    second[2 * columns :] += grown[columns // 2 :]
    small[6:7] += column_sum(dz1)


def attention_back_kernel(*refs):
    heads_ref, probs_ref, dz1_ref, wm_h, wm_l = refs[:5]
    back_h, back_l, dmixed_ref, dheads_ref = refs[-4:]
    nodes = dz1_ref.shape[1]
    rows = TOKENS * nodes
    columns = dz1_ref.shape[2]

    def by_token(values):
        return values.reshape(TOKENS, nodes, values.shape[-1])

    dz1 = split(dz1_ref[...].reshape(rows, columns))
    dmixed_ref[...] = by_token(product(dz1, pair(wm_h, wm_l), 1, 1))
    gather, spread = head_tables(columns)
    probs = probs_ref[...].reshape(TOKENS // 2 * nodes, LANES)
    dprobs = token_scores(
        lambda: dmixed_ref[...],
        lambda key: heads_ref[key, :, 2 * columns :],
        gather,
        nodes,
        columns,
    )
    dscores = probs * (dprobs - over_keys(probs * dprobs, jnp.add)) * (1.0 / math.sqrt(HEAD_DIM))
    for key in range(TOKENS):
        weight = by_token(one_key(probs, key, spread, nodes))
        dheads_ref[key, :, 2 * columns :] = jnp.sum(weight * dmixed_ref[...], axis=0)
        weight = by_token(one_key(dscores, key, spread, nodes))
        dheads_ref[key, :, columns : 2 * columns] = jnp.sum(
            weight * heads_ref[:, :, :columns], axis=0
        )
        term = weight * heads_ref[key, :, columns : 2 * columns][None]
        dheads_ref[:, :, :columns] = term if key == 0 else dheads_ref[:, :, :columns] + term
    back_h[...], back_l[...] = split(dheads_ref[...])


def input_back_kernel(
    hops_ref,
    z0_ref,
    back_h,
    back_l,
    dz1_ref,
    front_small,
    wi_h,
    wi_l,
    wh_h,
    wh_l,
    gain_attn,
    dhops_ref,
    sums,
):
    nodes = hops_ref.shape[1]
    rows = TOKENS * nodes
    columns = z0_ref.shape[2]
    features = hops_ref.shape[2]
    at_small = features + front_small.shape[0]

    @pl.when(pl.program_id(0) == 0)
    def _():
        sums[...] = jnp.zeros_like(sums)
        sums[features:at_small] = front_small[...]

    def flat(ref):
        return ref[...].reshape(rows, ref.shape[2])

    n1, scale = standard(flat(z0_ref))
    du1 = product((flat(back_h), flat(back_l)), pair(wh_h, wh_l), 1, 1)
    sums[at_small + 1 : at_small + 2] += column_sum(du1 * n1)
    sums[at_small + 2 : at_small + 3] += column_sum(du1)
    dz0 = flat(dz1_ref) + standard_back(du1 * gain_attn[...], n1, scale)
    sums[at_small + 3 : at_small + 4] += column_sum(dz0)
    near = split(dz0)
    sums[:features] += product(split(flat(hops_ref)), near, 0, 0)
    dhops_ref[...] = product(near, pair(wi_h, wi_l), 1, 1).reshape(TOKENS, nodes, features)


def heads_weight_kernel(z0_ref, back_h, back_l, rest, gain_attn, shift_attn, first, second, u_h, u_l):
    nodes = z0_ref.shape[1]
    rows = TOKENS * nodes
    columns = z0_ref.shape[2]

    @pl.when(pl.program_id(0) == 0)
    def _():
        first[...] = jnp.zeros_like(first)
        second[:columns] = jnp.zeros((columns, columns), jnp.float32)
        second[columns:] = rest[...]

    n1, _ = standard(z0_ref[...].reshape(rows, columns))
    u_h[...], u_l[...] = split(n1 * gain_attn[...] + shift_attn[...])
    for third in range(3):
        cut = slice(third * columns, (third + 1) * columns)
        grown = product(
            pair(u_h, u_l),
            (back_h[:, :, cut].reshape(rows, columns), back_l[:, :, cut].reshape(rows, columns)),
            0,
            0,
        )
        if third < 2:
            first[cut] += grown
        else:
            second[:columns] += grown


def split_kernel(*refs):
    count = len(refs) // 3
    for place in range(count):
        source, upper, lower = refs[place], refs[count + 2 * place], refs[count + 2 * place + 1]
        step = min(64, source.shape[0])

        def some(index, _, source=source, upper=upper, lower=lower, step=step):
            rows = pl.ds(pl.multiple_of(index * step, step), step)
            upper[rows, :], lower[rows, :] = split(source[rows, :])
            return 0

        lax.fori_loop(0, source.shape[0] // step, some, 0)


def layer_parts(hops, cotangent, w_input, bias_input, gain_attn, shift_attn, w_heads, w_merge, bias_merge, gain_ffn, shift_ffn, w_expand, bias_expand, w_reduce, bias_reduce, readout):
    tokens, node_count, features = hops.shape
    columns = w_input.shape[1]
    wide = w_expand.shape[1]
    nodes = min(NODES_STEP, node_count)
    rows = tokens * nodes
    f32, bf16 = jnp.float32, jnp.bfloat16

    def shape(*dims, dtype=f32):
        return jax.ShapeDtypeStruct(dims, dtype)

    weights = [w_input, w_heads, w_merge, w_expand, w_reduce]
    halves = pl.pallas_call(
        split_kernel,
        out_shape=[shape(*w.shape, dtype=bf16) for w in weights for _ in range(2)],
        compiler_params=pltpu.CompilerParams(vmem_limit_bytes=40 << 20),
        cost_estimate=work(4),
        name="split_weights",
    )(*weights)
    wi, wh, wm, we, wr = [halves[2 * i : 2 * i + 2] for i in range(5)]

    def fixed(array):
        return pl.BlockSpec(array.shape, lambda step: (0,) * len(array.shape), pipeline_mode=pl.Buffered(1))

    def row(vector):
        return vector.reshape(1, -1)

    def part(*dims):
        return pl.BlockSpec((dims[0], nodes, dims[1]), lambda step: (0, step, 0))

    flat = pl.BlockSpec((nodes, columns), lambda step: (step, 0))
    vectors = [row(v) for v in (bias_input, gain_attn, shift_attn, bias_merge, gain_ffn, shift_ffn, bias_expand, bias_reduce, readout)]
    outs = [
        shape(node_count, columns),
        shape(tokens, node_count, columns),
        shape(tokens, node_count, 3 * columns),
        shape(tokens // 2, node_count, LANES),
        shape(tokens, node_count, columns),
        shape(tokens, node_count, columns),
        shape(wide + columns // 2, columns),
        shape(2 * columns + columns // 2, columns),
        shape(8, columns),
    ]
    out, z0, heads, probs, _, dz1, first, second, front_small = pl.pallas_call(
        front_kernel,
        grid=(node_count // nodes,),
        out_shape=outs,
        in_specs=[part(tokens, features), flat]
        + [fixed(w) for w in (*wi, *wh, *wm, *we, *wr)]
        + [fixed(v) for v in vectors],
        out_specs=[
            flat,
            part(tokens, columns),
            part(tokens, 3 * columns),
            part(tokens // 2, LANES),
            part(tokens, columns),
            part(tokens, columns),
            fixed(outs[6]),
            fixed(outs[7]),
            fixed(outs[8]),
        ],
        scratch_shapes=[
            pltpu.VMEM((rows, columns), bf16),
            pltpu.VMEM((rows, columns), bf16),
            pltpu.VMEM((rows, wide), bf16),
            pltpu.VMEM((rows, wide), bf16),
            pltpu.VMEM((rows, wide), bf16),
            pltpu.VMEM((rows, wide), bf16),
            pltpu.VMEM((rows, wide), f32),
            pltpu.VMEM((rows, columns), f32),
            pltpu.VMEM((rows, columns), f32),
        ],
        compiler_params=pltpu.CompilerParams(vmem_limit_bytes=56 << 20),
        cost_estimate=work(52),
        name="layer_front",
    )(hops, cotangent, *wi, *wh, *wm, *we, *wr, *vectors)
    steps = node_count // nodes

    def attention_back(dz1, start, count, so_far):
        def some(*dims):
            return pl.BlockSpec((dims[0], nodes, dims[1]), lambda step: (0, step + start, 0))

        given = [heads, probs, dz1, *wm, *so_far]
        return pl.pallas_call(
            attention_back_kernel,
            grid=(count,),
            out_shape=[shape(tokens, node_count, 3 * columns, dtype=bf16)] * 2,
            in_specs=[
                some(tokens, 3 * columns),
                some(tokens // 2, LANES),
                some(tokens, columns),
                *[fixed(w) for w in wm],
                *[pl.BlockSpec(memory_space=pl.ANY) for _ in so_far],
            ],
            out_specs=[some(tokens, 3 * columns)] * 2,
            scratch_shapes=[
                pltpu.VMEM((tokens, nodes, columns), f32),
                pltpu.VMEM((tokens, nodes, 3 * columns), f32),
            ],
            input_output_aliases={5: 0, 6: 1} if so_far else {},
            compiler_params=pltpu.CompilerParams(vmem_limit_bytes=40 << 20),
            cost_estimate=work(5 * count),
            name="attention_back",
        )(*given)

    def input_back(back):
        given = [hops, z0, *back, dz1, front_small, *wi, *wh, vectors[1]]
        sums = shape(-(-(features + 16) // SHARE) * SHARE, columns)
        return pl.pallas_call(
            input_back_kernel,
            grid=(steps,),
            out_shape=[shape(tokens, node_count, features), sums],
            in_specs=[
                part(tokens, features),
                part(tokens, columns),
                part(tokens, 3 * columns),
                part(tokens, 3 * columns),
                part(tokens, columns),
                *[fixed(g) for g in given[5:]],
            ],
            out_specs=[part(tokens, features), fixed(sums)],
            compiler_params=pltpu.CompilerParams(vmem_limit_bytes=40 << 20),
            cost_estimate=work(10),
            name="input_back",
        )(*given)

    def heads_weight(back, rest):
        given = [z0, *back, rest, *vectors[1:3]]
        outs = [shape(2 * columns, columns), shape(columns + rest.shape[0], columns)]
        return pl.pallas_call(
            heads_weight_kernel,
            grid=(steps,),
            out_shape=outs,
            in_specs=[
                part(tokens, columns),
                part(tokens, 3 * columns),
                part(tokens, 3 * columns),
                *[fixed(g) for g in given[3:]],
            ],
            out_specs=[fixed(o) for o in outs],
            scratch_shapes=[pltpu.VMEM((rows, columns), bf16)] * 2,
            compiler_params=pltpu.CompilerParams(vmem_limit_bytes=40 << 20),
            cost_estimate=work(8),
            name="heads_weight",
        )(*given)

    return out, dz1, [first, second], steps, attention_back, input_back, heads_weight


CORE, Y, NEAR_Z, FAR_Z, X = ("row", 1), ("row", 2), ("row", 4), ("row", 8), ("col", 1)
ORDERS = ((CORE, X, Y, NEAR_Z, FAR_Z), (CORE, Y, X, NEAR_Z, FAR_Z))
SHARE = 256


def swap(values, stage):
    axis, distance = stage
    size = lax.axis_size(axis)
    return lax.ppermute(values, axis, [(place, place ^ distance) for place in range(size)])


def side(stage):
    axis, distance = stage
    return lax.axis_index(axis) // distance % 2


def tie(*values):
    return lax.optimization_barrier(values)


def halves(parts, step):
    kept, sent = [], []
    for part, order in zip(parts, ORDERS):
        half = part.shape[0] // 2
        mine = side(order[step])
        kept.append(lax.dynamic_slice_in_dim(part, mine * half, half))
        sent.append(lax.dynamic_slice_in_dim(part, (1 - mine) * half, half))
    return kept, sent


def swap_all(parts, step):
    return [swap(part, order[step]) for part, order in zip(parts, ORDERS)]


def add_all(left, right):
    return [a + b for a, b in zip(left, right)]


def reduce_step(parts, step):
    kept, sent = halves(parts, step)
    return add_all(kept, swap_all(sent, step))


def join_step(parts, step):
    return [jnp.concatenate([a, b], axis=0) for a, b in zip(parts, swap_all(parts, step))]


def last_join(parts):
    return [piece for both in zip(parts, swap_all(parts, 0)) for piece in both]


def part_places():
    found = []
    for order in ORDERS:
        place = jnp.int32(0)
        for stage in order:
            place = 2 * place + side(stage)
        found.append(place)
    return jnp.stack(found)


def gather_pieces(places_ref, pieces, whole):
    start = 0
    for part in range(2):
        count = 16
        size = pieces[2 * part].shape[0] // count
        for turn in range(2):
            for piece in range(count):
                target = ((turn * count + piece) ^ places_ref[part]) * size + start
                whole[pl.ds(pl.multiple_of(target, 8), size), :] = pieces[2 * part + turn][
                    piece * size : (piece + 1) * size
                ]
        start += 2 * count * size


def front_outputs(places_ref, *refs):
    pieces, (grad_reduce, grad_expand, grad_merge, whole) = refs[:4], refs[4:]
    gather_pieces(places_ref, pieces, whole)
    split_front(whole, grad_reduce, grad_expand, grad_merge)


def split_front(whole, grad_reduce, grad_expand, grad_merge):
    wide, columns = grad_reduce.shape
    part = columns // 2
    grad_reduce[...] = whole[:wide]
    grad_merge[:part] = whole[wide : wide + part]
    start = wide + part
    grad_expand[:, :columns] = whole[start : start + columns]
    grad_expand[:, columns:] = whole[start + columns : start + 2 * columns]
    grad_merge[part:] = whole[start + 2 * columns :]


def back_outputs(places_ref, *refs):
    pieces, whole = refs[:4], refs[-1]
    gather_pieces(places_ref, pieces, whole)
    split_back(whole, *refs[4:-1])


def split_back(whole, grad_heads, grad_input, *vectors):
    columns = grad_heads.shape[0]
    for third in range(3):
        grad_heads[:, third * columns : (third + 1) * columns] = whole[
            third * columns : (third + 1) * columns
        ]
    start = 3 * columns
    grad_input[...] = whole[start : start + grad_input.shape[0]]
    start += grad_input.shape[0]
    for vector, row in zip(vectors, SMALL_ROWS):
        vector[:, :columns] = whole[start + row : start + row + 1]
    vectors[2][:, columns:] = whole[start + 5 : start + 6]


SMALL_ROWS = (0, 1, 2, 3, 4, 6, 9, 10, 11)


def outputs(kernel, name, places, pieces, shapes, rows, columns):
    return pl.pallas_call(
        kernel,
        out_shape=[jax.ShapeDtypeStruct(s, jnp.float32) for s in shapes],
        in_specs=[pl.BlockSpec(memory_space=pltpu.SMEM)]
        + [pl.BlockSpec(memory_space=pltpu.VMEM)] * len(pieces),
        out_specs=[pl.BlockSpec(memory_space=pltpu.VMEM)] * len(shapes),
        scratch_shapes=[pltpu.VMEM((rows, columns), jnp.float32)],
        compiler_params=pltpu.CompilerParams(vmem_limit_bytes=48 << 20),
        cost_estimate=work(4),
        name=name,
    )(places, *pieces)


def join_two(first, second, whole):
    whole[: first.shape[0]] = first[...]
    whole[first.shape[0] :] = second[...]


def front_whole(places_ref, first, second, *refs):
    join_two(first, second, refs[-1])
    split_front(refs[-1], *refs[:-1])


def back_whole(places_ref, first, second, *refs):
    join_two(first, second, refs[-1])
    split_back(refs[-1], *refs[:-1])


def per_device(
    node_features,
    block_values,
    block_rows,
    block_cols,
    block_count,
    w_input,
    bias_input,
    gain_attn,
    shift_attn,
    w_heads,
    w_merge,
    bias_merge,
    gain_ffn,
    shift_ffn,
    w_expand,
    bias_expand,
    w_reduce,
    bias_reduce,
    readout,
    cotangent,
):
    values = block_values[0, 0]
    row_ids = block_rows[0, 0]
    col_ids = block_cols[0, 0]
    block_size = values.shape[-1]
    node_count = node_features.shape[0]
    row_blocks = lax.axis_size("col") * node_count // block_size
    col_blocks = lax.axis_size("row") * node_count // block_size
    is_live = (jnp.arange(values.shape[0]) < block_count[0, 0]).astype(jnp.float32)
    row_table = (row_ids[:, None] == jnp.arange(row_blocks)[None, :]).astype(jnp.float32) * is_live[
        :, None
    ]
    col_table = (col_ids[:, None] == jnp.arange(col_blocks)[None, :]).astype(jnp.float32) * is_live[
        :, None
    ]
    devices = lax.axis_size("row") * lax.axis_size("col")
    whole = (
        block_size == LANES
        and node_count == LANES
        and node_features.shape[1] == PIECE * devices
        and devices * values.size * 4 <= 16 << 20
    )
    if whole:
        n_col = lax.axis_size("col")
        everything = lax.all_gather(values, AXES, axis=0, tiled=True)
        places = jnp.concatenate([row_ids, col_ids, block_count[0]]).astype(jnp.float32)
        note = jnp.zeros((PIECE, LANES), jnp.float32).at[0, : places.shape[0]].set(places)
        sent = jnp.concatenate(
            [
                node_features.T.reshape(devices, PIECE, LANES),
                jnp.broadcast_to(note[None], (devices, PIECE, LANES)),
            ],
            axis=1,
        )
        taken = lax.all_to_all(sent, AXES, 0, 0, tiled=True)
        meta = taken[:, PIECE, : places.shape[0]].astype(jnp.int32)
        walked = walk(True, meta, taken, everything, n_col, row_blocks)
        walked = lax.all_to_all(walked, AXES, 0, 0, tiled=True)
        stacked = walked.reshape(devices, TOKENS, PIECE, LANES).transpose(1, 3, 0, 2)
        stacked = stacked.reshape(TOKENS, LANES, devices * PIECE)
    else:
        hop_list = [node_features]
        for hop_index in range(HOPS):
            field = hop_list[-1]
            forward_columns = field.shape[1]
            forward_gathered = lax.all_gather(field, "row", axis=0, tiled=True).reshape(
                col_blocks, block_size, forward_columns
            )
            forward_picked = forward_gathered[col_ids]
            forward_products = jnp.einsum("bij,bjw->biw", values, forward_picked, precision=exact)
            forward_partial_value = jnp.einsum(
                "br,biw->riw", row_table, forward_products, precision=exact
            ).reshape(row_blocks * block_size, forward_columns)
            hop_list.append(
                lax.psum_scatter(forward_partial_value, "col", scatter_dimension=0, tiled=True)
            )
        stacked = jnp.stack(hop_list, axis=0)

    layer_out, dz1, front, steps, attention_back, input_back, heads_weight = layer_parts(
        stacked,
        cotangent,
        w_input,
        bias_input,
        gain_attn,
        shift_attn,
        w_heads,
        w_merge,
        bias_merge,
        gain_ffn,
        shift_ffn,
        w_expand,
        bias_expand,
        w_reduce,
        bias_reduce,
        readout,
    )
    columns, wide = w_expand.shape
    if whole and lax.axis_size("row") == 16 and n_col == 2:
        kept, sent = halves(front, 0)
        sent, dz1 = tie(sent, dz1)
        taken = swap_all(sent, 0)
        early = attention_back(dz1, 0, steps // 2, ())
        kept, taken, early = tie(kept, taken, early)
        kept, sent = halves(add_all(kept, taken), 1)
        sent, dz1, early = tie(sent, dz1, early)
        taken = swap_all(sent, 1)
        back = attention_back(dz1, steps // 2, steps - steps // 2, early)
        grad_hops, rest = input_back(back)
        kept, taken, grad_hops, rest = tie(kept, taken, grad_hops, rest)
        kept, sent = halves(add_all(kept, taken), 2)
        away = grad_hops.reshape(TOKENS, LANES, devices, PIECE).transpose(2, 0, 3, 1)
        away = away.reshape(devices, TOKENS * PIECE, LANES)
        sent, away, back = tie(sent, away, back)
        taken = swap_all(sent, 2)
        away = lax.all_to_all(away, AXES, 0, 0, tiled=True)
        late = heads_weight(back, rest)
        kept, taken, late = tie(kept, taken, late)
        front = add_all(kept, taken)
        front = reduce_step(front, 3)
        late = reduce_step(late, 0)
        kept, sent = halves(front, 4)
        late_kept, late_sent = halves(late, 1)
        sent, late_sent, away = tie(sent, late_sent, away)
        taken, late_taken = swap_all(sent, 4), swap_all(late_sent, 1)
        home = walk(False, meta, away, everything, n_col, row_blocks)
        taken, late_taken, home = tie(taken, late_taken, home)
        home = lax.all_to_all(home, AXES, 0, 0, tiled=True)[:, :PIECE]
        carried = grad_hops[0] + home.reshape(devices * PIECE, LANES).T
        front = add_all(kept, taken)
        late = add_all(late_kept, late_taken)
        for step in (2, 3, 4):
            late = reduce_step(late, step)
        for step in (4, 3, 2, 1):
            front = join_step(front, step)
            late = join_step(late, step)
        front, late, order = last_join(front), last_join(late), part_places()
        kernels = front_outputs, back_outputs
    else:
        back = attention_back(dz1, 0, steps, ())
        grad_hops, rest = input_back(back)
        late = heads_weight(back, rest)
        carried = grad_hops[HOPS]
        for hop_index in range(HOPS - 1, -1, -1):
            gathered = lax.all_gather(carried, "col", axis=0, tiled=True).reshape(
                row_blocks, block_size, carried.shape[1]
            )
            picked = gathered[row_ids]
            products = jnp.einsum("bji,bjw->biw", values, picked, precision=exact)
            partial_value = jnp.einsum("bc,biw->ciw", col_table, products, precision=exact)
            carried = grad_hops[hop_index] + lax.psum_scatter(
                partial_value.reshape(col_blocks * block_size, carried.shape[1]),
                "row",
                scatter_dimension=0,
                tiled=True,
            )
        front, late = lax.psum((front, late), AXES)
        order = jnp.zeros((2,), jnp.int32)
        kernels = front_whole, back_whole
    front_shapes = [(wide, columns), (columns, wide), (columns, columns)]
    back_shapes = [(columns, 3 * columns), w_input.shape]
    back_shapes += [(1, wide if row == 2 else columns) for row in SMALL_ROWS]
    front_rows = wide + 3 * columns
    back_rows = 3 * columns + rest.shape[0]
    grad_w_reduce, grad_w_expand, grad_w_merge = outputs(
        kernels[0], "front_outputs", order, front, front_shapes, front_rows, columns
    )
    grad_w_heads, grad_w_input, *vectors = outputs(
        kernels[1], "back_outputs", order, late, back_shapes, back_rows, columns
    )
    (
        grad_readout,
        grad_bias_reduce,
        grad_bias_expand,
        grad_gain_ffn,
        grad_shift_ffn,
        grad_bias_merge,
        grad_gain_attn,
        grad_shift_attn,
        grad_bias_input,
    ) = [vector.reshape(-1) for vector in vectors]
    return (
        layer_out,
        carried,
        grad_w_input,
        grad_bias_input,
        grad_gain_attn,
        grad_shift_attn,
        grad_w_heads,
        grad_w_merge,
        grad_bias_merge,
        grad_gain_ffn,
        grad_shift_ffn,
        grad_w_expand,
        grad_bias_expand,
        grad_w_reduce,
        grad_bias_reduce,
        grad_readout,
    )


def solution(mesh):
    placed = (
        P(("row", "col"), None),
        P("row", "col", None, None, None),
        P("row", "col", None),
        P("row", "col", None),
        P("row", "col"),
        P(),
        P(),
        P(),
        P(),
        P(),
        P(),
        P(),
        P(),
        P(),
        P(),
        P(),
        P(),
        P(),
        P(),
        P(("row", "col"), None),
    )
    return jax.shard_map(
        per_device,
        mesh=mesh,
        in_specs=placed,
        out_specs=(
            P(("row", "col"), None),
            P(("row", "col"), None),
            P(),
            P(),
            P(),
            P(),
            P(),
            P(),
            P(),
            P(),
            P(),
            P(),
            P(),
            P(),
            P(),
            P(),
        ),
        check_vma=False,
    )
```

time: 583 us -> 386 us (0.66); the launches traced: 571 us -> 385 us
  matrix products: 146 us -> 0 us
  Pallas kernels: 54.2 us -> 131 us
  waiting for transfers between devices: 173 us -> 109 us
  blocking collectives: 75.3 us -> 15.8 us
  starting transfers between devices: 6.43 us -> 61.9 us
  local copies, waits for them, and re-layouts: 75.9 us -> 42.8 us
  other arithmetic: 24.4 us -> 9.31 us
    dot_general x25 -> x0, matrix products: 146 us -> none  [the longest x3 32.4 us: node_tail(): projected = jnp.einsum('ntd,de->nte', normed, w_heads, precision=near)]
    pallas_call x0 -> x8, Pallas kernels: none -> 103 us  [the longest x1 53.2 us: layer_parts(): pl.pallas_call(front_kernel, grid=(node_count // nodes,), out_shape=outs,...]
    psum x1 -> x0, waiting for transfers between devices: 87.9 us -> none  [per_device(): lax.psum((grad_w_input, grad_bias_input, grad_gain_attn, grad_shift_attn,...]
    ppermute x0 -> x40, starting transfers between devices: none -> 47.6 us  [swap(): lax.ppermute(values, axis, [(place, place ^ distance) for place in range(...]
    psum x1 -> x0, blocking collectives: 41.5 us -> none  [per_device(): lax.psum((grad_w_input, grad_bias_input, grad_gain_attn, grad_shift_attn,...]
    ppermute x0 -> x40, waiting for transfers between devices: none -> 34.8 us  [swap(): lax.ppermute(values, axis, [(place, place ^ distance) for place in range(...]
    pallas_call x2, Pallas kernels: 54.2 us -> 28.1 us  [walk(): pl.pallas_call(functools.partial(walk_kernel, forward, HOPS, slots, n_col...]
    transpose x5 -> x1, local copies, waits for them, and re-layouts: 25 us -> 2.12 us  [per_device(): grad_hops.reshape(TOKENS, LANES, devices, PIECE).transpose(2, 0, 3, 1)]
  transfers between devices with their start and end apart: 4 -> 44, of which waited for: 3 -> 16; matrix products, arithmetic and copies ran while one was open for 3% -> 4% of each run, Pallas kernels for 4% -> 15%
where the time goes in v2:
time: 386 us; the launch traced here: 385 us
  Pallas kernels  131 us (34%)
  waiting for transfers between devices  109 us (28%)
  starting transfers between devices  61.9 us (16%)
  local copies, waits for them, and re-layouts  42.8 us (11%)
  blocking collectives  15.8 us (4%)
  between operations  15.5 us (4%)
  other arithmetic  9.31 us (2%)
    all_gather x1, waiting for transfers between devices, per_device(): everything = lax.all_gather(values, AXES, axis=0, tiled=True)  64.8 us
    pallas_call x1, Pallas kernels, layer_parts(): pl.pallas_call(front_kernel, grid=(node_count // nodes,), out_shape=outs,...  53.2 us
    ppermute x40, starting transfers between devices, swap(): lax.ppermute(values, axis, [(place, place ^ distance) for place in range(...  47.6 us
    ppermute x40, waiting for transfers between devices, swap(): lax.ppermute(values, axis, [(place, place ^ distance) for place in range(...  34.8 us
    pallas_call x2, Pallas kernels, walk(): pl.pallas_call(functools.partial(walk_kernel, forward, HOPS, slots, n_col...  28.1 us
    unnamed x101, local copies, waits for them, and re-layouts  26.1 us
    pallas_call x2, Pallas kernels, attention_back(): pl.pallas_call(attention_back_kernel, grid=(count,), out_shape=[shape(tok...  17.9 us
    all_to_all x1, blocking collectives, per_device(): taken = lax.all_to_all(sent, AXES, 0, 0, tiled=True)  15.8 us
  transfers between devices with their start and end apart: 44, of which 16 were waited for; matrix products, arithmetic and copies ran while one was open for 4% of the time, Pallas kernels for 15%

profile of v2, /device:TPU:0, one launch (start us, length us, event | category | flops | bytes accessed | tf_op | source)
XLA Modules:
  0.0 385.1 jit_solution(2355976841395149116)
XLA Ops:
  10.3 15.8 %all_to_all.20.field_ref = f32[32,8,128]{2,1,0:T(8,128)S(1)} all-to-all(f32[32,8,128]{2,1,0:T(8,128)S(1)} %pad_maximum_fusion.10), channel_id=1, replica_groups=mesh['row'=16,'col'=2] {'row','col'}, dimensions={0} | all-to-all | bytes 262144 | tf_op jit(solution)/shard_map/all_to_all | solution.py:838
  26.2 64.8 %all-gather.3.cloned.1.call-done = f32[1,1,128,128,128]{4,3,1,0,2:T(8,128)} async-done(((f32[1,1,4,128,128]{4,3,1,0,2:T(8,128)}), f32[1,1,128,128,128]{4,3,1,0,2:T(8,128)}) %all-gather.3.cloned.1.call-update) | async-done | bytes 8388624 | tf_op jit(solution)/shard_map/all_gather | solution.py:828
  91.0 15.1 %walk_forward.1 = f32[32,32,128]{2,1,0:T(8,128)} custom-call(s32[32,9]{1,0:T(8,128)S(1)} %convert_bitcast_fusion.meta_ref, f32[32,8,128]{2,1,0:T(8,128)S(1)} %all_to_all.20.field_ref, f32[128,128,128]{2,1,0:T(8,128)} %bitcast.58), custom_call_target="tpu_custom_call" | custom-call | flops 20000000000 | bytes 60000000 | tf_op jit(solution)/shard_map/walk_forward/pallas_call | solution.py:116
  106.1 3.4 all-to-all-start.1
  112.3 3.3 split_weights.1
  126.0 53.2 %layer_front.1 = (f32[128,512]{1,0:T(8,128)}, f32[8,128,512]{2,1,0:T(8,128)}, f32[8,128,1536]{2,1,0:T(8,128)}, f32[4,128,128]{2,1,0:T(8,128)}, f32[8,128,512]{2,...) custom-call(f32[8,128,128]{2,1,0:T(8,128)} %copy.55.hops_ref, ...), custom_call_target="tpu_custom_call" | custom-call | flops 51999997952 | bytes 156000000 | tf_op jit(solution)/shard_map/layer_front/pallas_call | solution.py:533
  179.2 5.1 %constant_dynamic-slice_fusion.22 = (f32[640,512]{1,0:T(8,128)}, f32[640,512]{1,0:T(8,128)}, f32[640,512]{1,0:T(8,128)}, f32[640,512]{1,0:T(8,128)}) fusion(f32[1280,512]{1,0:T(8,128)} %get-tuple-element.121, s32[]{:T(128)S(6)} %select_n.220, s32[]{:T(128)S(6)} %select_n.219, f32[1280,512]{1,0:T(8,128)} %get-tuple-element.120), kind=kLoop, calls=%fused_computation.71 | loop fusion | bytes 10485768 | tf_op jit(solution)/shard_map/dynamic_slice | solution.py:665
  184.9 9.1 %attention_back.2 = (bf16[8,128,1536]{2,1,0:T(8,128)(2,1)S(1)}, bf16[8,128,1536]{2,1,0:T(8,128)(2,1)S(1)}) custom-call(f32[8,128,1536]{2,1,0:T(8,128)} %get-tuple-element.125.refs_0_, f32[4,128,128]{2,1,0:T(8,128)S(1)} %copy-done.32, f32[8,128,512]{2,1,0:T(8,128)S(1)} %copy-done.24, bf16[512,512]{1,0:T(8,128)(2,1)S(1)} %copy-done.16, ...), custom_call_target="tpu_custom_call" | custom-call | flops 10000000000 | bytes 30000000 | tf_op jit(solution)/shard_map/attention_back/pallas_call | solution.py:573
  202.4 8.8 %attention_back.3 = (bf16[8,128,1536]{2,1,0:T(8,128)(2,1)S(1)}, bf16[8,128,1536]{2,1,0:T(8,128)(2,1)S(1)}) custom-call(f32[8,128,1536]{2,1,0:T(8,128)} %get-tuple-element.125.refs_0_, f32[4,128,128]{2,1,0:T(8,128)S(1)} %copy-done.32, f32[8,128,512]{2,1,0:T(8,128)S(1)} %copy-done.25, ...), custom_call_target="tpu_custom_call", output_to_operand_aliasing={{0}: (5, {}), {1}: (6, {})} | custom-call | flops 10000000000 | bytes 30000000 | tf_op jit(solution)/shard_map/attention_back/pallas_call | solution.py:573
  212.9 12.2 %input_back.1 = (f32[8,128,128]{2,1,0:T(8,128)S(1)}, f32[256,512]{1,0:T(8,128)S(1)}) custom-call(f32[8,128,128]{2,1,0:T(8,128)S(1)} %copy-done, f32[8,128,512]{2,1,0:T(8,128)S(1)} %copy-done.23, bf16[8,128,1536]{2,1,0:T(8,128)(2,1)S(1)} %get-tuple-element.154.back_h, bf16[8,128,1536]{2,1,0:T(8,128)(2,1)} %copy-done.21, f32[8,128,512]{2,1,0:T(8,128)S(1)} %copy-done.25, ...), custom_call_target="tpu_custom_call" | custom-call | flops 10000000000 | bytes 30000000 | tf_op jit(solution)/shard_map/input_back/pallas_call | solution.py:598
  234.3 5.4 %all-to-all-start.2 = ((f32[32,32,128]{2,1,0:T(8,128)}), f32[32,32,128]{2,1,0:T(8,128)S(1)}, u32[]{:S(2)}, u32[]{:S(2)}) async-start(f32[32,32,128]{2,1,0:T(8,128)} %bitcast.48), calls=%async_computation.2 | async-start | bytes 1048576 | tf_op jit(solution)/shard_map/all_to_all | solution.py:898
  244.6 7.4 %heads_weight.1 = (f32[1024,512]{1,0:T(8,128)S(1)}, f32[768,512]{1,0:T(8,128)S(1)}) custom-call(f32[8,128,512]{2,1,0:T(8,128)S(1)} %copy-done.23, bf16[8,128,1536]{2,1,0:T(8,128)(2,1)S(1)} %copy-done.20, bf16[8,128,1536]{2,1,0:T(8,128)(2,1)S(1)} %copy-done.22, f32[256,512]{1,0:T(8,128)S(1)} %copy-done.31, f32[1,512]{1,0:T(1,128)S(1)} %bitcast.45, ...), custom_call_target="tpu_custom_call" | custom-call | flops 8000000000 | bytes 24000000 | tf_op jit(solution)/shard_map/heads_weight/pallas_call | solution.py:619
  257.1 3.2 collective-permute-done.6
  260.3 2.5 collective-permute-done.7
  264.9 2.6 collective-permute-start.10
  270.9 13.0 %walk_backward.1 = f32[32,8,128]{2,1,0:T(8,128)} custom-call(s32[32,9]{1,0:T(8,128)S(1)} %convert_bitcast_fusion.meta_ref, f32[32,32,128]{2,1,0:T(8,128)S(1)} %all-to-all-done.2.field_ref, f32[128,128,128]{2,1,0:T(8,128)} %bitcast.59), custom_call_target="tpu_custom_call" | custom-call | flops 20000000000 | bytes 60000000 | tf_op jit(solution)/shard_map/walk_backward/pallas_call | solution.py:116
  285.3 2.6 collective-permute-start.30
  288.4 4.2 %collective-permute-done.30 = f32[40,512]{1,0:T(8,128)S(1)} collective-permute-done((f32[40,512]{1,0:T(8,128)S(1)}, f32[40,512]{1,0:T(8,128)S(1)}, u32[]{:S(2)}, u32[]{:S(2)}) %collective-permute-start.30) | collective-permute-done | bytes 81952 | tf_op jit(solution)/shard_map/ppermute | solution.py:647
  293.4 2.4 collective-permute-start.36
  296.0 2.8 collective-permute-done.31
  302.2 2.4 collective-permute-start.24
  304.6 2.5 collective-permute-start.15
  308.4 2.1 collective-permute-start.25
  313.4 2.6 collective-permute-start.26
  318.0 2.6 collective-permute-start.17
  331.9 5.6 %collective-permute-done.19 = f32[128,512]{1,0:T(8,128)S(1)} collective-permute-done((f32[128,512]{1,0:T(8,128)S(1)}, f32[128,512]{1,0:T(8,128)S(1)}, u32[]{:S(2)}, u32[]{:S(2)}) %collective-permute-start.19) | collective-permute-done | bytes 262176 | tf_op jit(solution)/shard_map/ppermute | solution.py:647
  342.0 4.0 %collective-permute-done.33 = f32[320,512]{1,0:T(8,128)S(1)} collective-permute-done((f32[320,512]{1,0:T(8,128)S(1)}, f32[320,512]{1,0:T(8,128)S(1)}, u32[]{:S(2)}, u32[]{:S(2)}) %collective-permute-start.33) | collective-permute-done | bytes 655392 | tf_op jit(solution)/shard_map/ppermute | solution.py:647
  346.1 5.5 %collective-permute-done.20 = f32[256,512]{1,0:T(8,128)S(1)} collective-permute-done((f32[256,512]{1,0:T(8,128)S(1)}, f32[256,512]{1,0:T(8,128)S(1)}, u32[]{:S(2)}, u32[]{:S(2)}) %collective-permute-start.20) | collective-permute-done | bytes 524320 | tf_op jit(solution)/shard_map/ppermute | solution.py:647
  354.6 5.5 %all-to-all-start.3 = ((f32[32,8,128]{2,1,0:T(8,128)}), f32[32,8,128]{2,1,0:T(8,128)S(1)}, u32[]{:S(2)}, u32[]{:S(2)}) async-start(f32[32,8,128]{2,1,0:T(8,128)} %walk_backward.1), calls=%async_computation.3 | async-start | bytes 262144 | tf_op jit(solution)/shard_map/all_to_all | solution.py:910
  360.2 8.5 %all-to-all-done.3 = f32[32,8,128]{2,1,0:T(8,128)S(1)} async-done(((f32[32,8,128]{2,1,0:T(8,128)}), f32[32,8,128]{2,1,0:T(8,128)S(1)}, u32[]{:S(2)}, u32[]{:S(2)}) %all-to-all-start.3) | async-done | bytes 131104 | tf_op jit(solution)/shard_map/all_to_all | solution.py:910
  369.5 4.1 %back_outputs.1 = (f32[512,1536]{1,0:T(8,128)}, f32[128,512]{1,0:T(8,128)}, f32[1,512]{1,0:T(1,128)}, f32[1,512]{1,0:T(1,128)}, f32[1,1024]{1,0:T(1,128)}, /*ind...) custom-call(s32[2]{0:T(128)S(1)} %pad_add_fusion.places_ref, ...), custom_call_target="tpu_custom_call" | custom-call | flops 4000000000 | bytes 12000000 | tf_op jit(solution)/shard_map/back_outputs/pallas_call | solution.py:755
  373.7 4.6 %front_outputs.1 = (f32[1024,512]{1,0:T(8,128)}, f32[512,1024]{1,0:T(8,128)}, f32[512,512]{1,0:T(8,128)}) custom-call(s32[2]{0:T(128)S(1)} %pad_add_fusion.places_ref, f32[640,512]{1,0:T(8,128)S(1)} %constant_dynamic-update-slice_fusion.10.refs_0_, f32[640,512]{1,0:T(8,128)} %collective-permute-done.34.refs_1_, ...), custom_call_target="tpu_custom_call" | custom-call | flops 4000000000 | bytes 12000000 | tf_op jit(solution)/shard_map/front_outputs/pallas_call | solution.py:755
  (238 shorter events, 82.6 us)
Async XLA Ops:
  7.2 83.8 %all-gather.3.cloned.1.call-start = ((), (), s32[]{:S(2)}) async-start(), calls=%async_computation.4 | async-start | bytes 8650752 | tf_op jit(solution)/shard_map/all_gather | solution.py:828
  106.1 18.9 %all-to-all-start.1 = ((f32[32,32,128]{2,1,0:T(8,128)}), f32[32,32,128]{2,1,0:T(8,128)S(1)}, u32[]{:S(2)}, u32[]{:S(2)}) async-start(f32[32,32,128]{2,1,0:T(8,128)} %walk_forward.1), calls=%async_computation.1 | async-start | bytes 1048576 | tf_op jit(solution)/shard_map/all_to_all | solution.py:841
  184.4 9.7 %collective-permute-start = (f32[640,512]{1,0:T(8,128)}, f32[640,512]{1,0:T(8,128)}, u32[]{:S(2)}, u32[]{:S(2)}) collective-permute-start(f32[640,512]{1,0:T(8,128)} %get-tuple-element.123), channel_id=1, source_target_pairs={{0,2},{2,0},{4,6},{6,4},{8,10},{10,8},{12,14},{14,12},{16,18},{18,... | collective-permute-start | bytes 3932168 | tf_op jit(solution)/shard_map/ppermute | solution.py:647
  184.8 9.3 %collective-permute-start.1 = (f32[640,512]{1,0:T(8,128)}, f32[640,512]{1,0:T(8,128)}, u32[]{:S(2)}, u32[]{:S(2)}) collective-permute-start(f32[640,512]{1,0:T(8,128)} %get-tuple-element.124), channel_id=1, source_target_pairs={{0,2},{2,0},{4,6},{6,4},{8,10},{10,8},{12,14},{14,12},{16,18},{18,... | collective-permute-start | bytes 3932168 | tf_op jit(solution)/shard_map/ppermute | solution.py:647
  199.3 26.7 %collective-permute-start.2 = (f32[320,512]{1,0:T(8,128)S(1)}, f32[320,512]{1,0:T(8,128)S(1)}, u32[]{:S(2)}, u32[]{:S(2)}) collective-permute-start(f32[320,512]{1,0:T(8,128)S(1)} %get-tuple-element.136), channel_id=1, source_target_pairs={{0,1},{1,0},{2,3},{3,2},{4,5},{5,4},{6,7},{7,6},{8,9},{9,8},{10,11... | collective-permute-start | bytes 1966088 | tf_op jit(solution)/shard_map/ppermute | solution.py:647
  201.0 25.8 %collective-permute-start.3 = (f32[320,512]{1,0:T(8,128)S(1)}, f32[320,512]{1,0:T(8,128)S(1)}, u32[]{:S(2)}, u32[]{:S(2)}) collective-permute-start(f32[320,512]{1,0:T(8,128)S(1)} %get-tuple-element.137), channel_id=1, source_target_pairs={{0,4},{2,6},{4,0},{6,2},{8,12},{10,14},{12,8},{14,10},{16,20},{18,... | collective-permute-start | bytes 1966088 | tf_op jit(solution)/shard_map/ppermute | solution.py:647
  232.8 19.2 %collective-permute-start.4 = (f32[160,512]{1,0:T(8,128)}, f32[160,512]{1,0:T(8,128)}, u32[]{:S(2)}, u32[]{:S(2)}) collective-permute-start(f32[160,512]{1,0:T(8,128)} %get-tuple-element.152), channel_id=1, source_target_pairs={{0,4},{2,6},{4,0},{6,2},{8,12},{10,14},{12,8},{14,10},{16,20},{18,... | collective-permute-start | bytes 983048 | tf_op jit(solution)/shard_map/ppermute | solution.py:647
  233.4 18.7 %collective-permute-start.5 = (f32[160,512]{1,0:T(8,128)}, f32[160,512]{1,0:T(8,128)}, u32[]{:S(2)}, u32[]{:S(2)}) collective-permute-start(f32[160,512]{1,0:T(8,128)} %get-tuple-element.153), channel_id=1, source_target_pairs={{0,1},{1,0},{2,3},{3,2},{4,5},{5,4},{6,7},{7,6},{8,9},{9,8},{10,11... | collective-permute-start | bytes 983048 | tf_op jit(solution)/shard_map/ppermute | solution.py:647
  234.3 30.6 %all-to-all-start.2 = ((f32[32,32,128]{2,1,0:T(8,128)}), f32[32,32,128]{2,1,0:T(8,128)S(1)}, u32[]{:S(2)}, u32[]{:S(2)}) async-start(f32[32,32,128]{2,1,0:T(8,128)} %bitcast.48), calls=%async_computation.2 | async-start | bytes 1048576 | tf_op jit(solution)/shard_map/all_to_all | solution.py:898
  253.1 7.1 %collective-permute-start.6 = (f32[80,512]{1,0:T(8,128)S(1)}, f32[80,512]{1,0:T(8,128)S(1)}, u32[]{:S(2)}, u32[]{:S(2)}) collective-permute-start(f32[80,512]{1,0:T(8,128)S(1)} %constant_dynamic-slice_fusion.13), channel_id=1, source_target_pairs={{0,8},{2,10},{4,12},{6,14},{8,0},{10,2},{12,4},{14,6},{16,24},{18,... | collective-permute-start | bytes 491528 | tf_op jit(solution)/shard_map/ppermute | solution.py:647
  256.5 7.3 %collective-permute-start.8 = (f32[512,512]{1,0:T(8,128)S(1)}, f32[512,512]{1,0:T(8,128)S(1)}, u32[]{:S(2)}, u32[]{:S(2)}) collective-permute-start(f32[512,512]{1,0:T(8,128)S(1)} %constant_dynamic-slice_fusion.9), channel_id=1, source_target_pairs={{0,2},{2,0},{4,6},{6,4},{8,10},{10,8},{12,14},{14,12},{16,18},{18,... | collective-permute-start | bytes 3145736 | tf_op jit(solution)/shard_map/ppermute | solution.py:647
  264.9 19.1 %collective-permute-start.10 = (f32[40,512]{1,0:T(8,128)S(1)}, f32[40,512]{1,0:T(8,128)S(1)}, u32[]{:S(2)}, u32[]{:S(2)}) collective-permute-start(f32[40,512]{1,0:T(8,128)S(1)} %constant_dynamic-slice_fusion.12), channel_id=1, source_target_pairs={{0,16},{2,18},{4,20},{6,22},{8,24},{10,26},{12,28},{14,30},{16,0},... | collective-permute-start | bytes 245768 | tf_op jit(solution)/shard_map/ppermute | solution.py:647
  267.4 16.5 %collective-permute-start.11 = (f32[40,512]{1,0:T(8,128)S(1)}, f32[40,512]{1,0:T(8,128)S(1)}, u32[]{:S(2)}, u32[]{:S(2)}) collective-permute-start(f32[40,512]{1,0:T(8,128)S(1)} %constant_dynamic-slice_fusion.10), channel_id=1, source_target_pairs={{0,16},{2,18},{4,20},{6,22},{8,24},{10,26},{12,28},{14,30},{16,0},... | collective-permute-start | bytes 245768 | tf_op jit(solution)/shard_map/ppermute | solution.py:647
  267.8 16.2 %collective-permute-start.12 = (f32[256,512]{1,0:T(8,128)}, f32[256,512]{1,0:T(8,128)S(1)}, u32[]{:S(2)}, u32[]{:S(2)}) collective-permute-start(f32[256,512]{1,0:T(8,128)} %constant_dynamic-slice_fusion.8), channel_id=1, source_target_pairs={{0,1},{1,0},{2,3},{3,2},{4,5},{5,4},{6,7},{7,6},{8,9},{9,8},{10,11... | collective-permute-start | bytes 1572872 | tf_op jit(solution)/shard_map/ppermute | solution.py:647
  269.5 14.5 %collective-permute-start.13 = (f32[192,512]{1,0:T(8,128)}, f32[192,512]{1,0:T(8,128)S(1)}, u32[]{:S(2)}, u32[]{:S(2)}) collective-permute-start(f32[192,512]{1,0:T(8,128)} %constant_dynamic-slice_fusion.6), channel_id=1, source_target_pairs={{0,4},{2,6},{4,0},{6,2},{8,12},{10,14},{12,8},{14,10},{16,20},{18,... | collective-permute-start | bytes 1179656 | tf_op jit(solution)/shard_map/ppermute | solution.py:647
  284.1 18.0 %collective-permute-start.14 = (f32[128,512]{1,0:T(8,128)S(1)}, f32[128,512]{1,0:T(8,128)S(1)}, u32[]{:S(2)}, u32[]{:S(2)}) collective-permute-start(f32[128,512]{1,0:T(8,128)S(1)} %constant_dynamic-slice_fusion.5), channel_id=1, source_target_pairs={{0,4},{2,6},{4,0},{6,2},{8,12},{10,14},{12,8},{14,10},{16,20},{18,... | collective-permute-start | bytes 786440 | tf_op jit(solution)/shard_map/ppermute | solution.py:647
  284.8 11.0 %collective-permute-start.22 = (f32[96,512]{1,0:T(8,128)S(1)}, f32[96,512]{1,0:T(8,128)S(1)}, u32[]{:S(2)}, u32[]{:S(2)}) collective-permute-start(f32[96,512]{1,0:T(8,128)S(1)} %constant_dynamic-slice_fusion.2), channel_id=1, source_target_pairs={{0,1},{1,0},{2,3},{3,2},{4,5},{5,4},{6,7},{7,6},{8,9},{9,8},{10,11... | collective-permute-start | bytes 589832 | tf_op jit(solution)/shard_map/ppermute | solution.py:647
  285.3 7.2 %collective-permute-start.30 = (f32[40,512]{1,0:T(8,128)S(1)}, f32[40,512]{1,0:T(8,128)S(1)}, u32[]{:S(2)}, u32[]{:S(2)}) collective-permute-start(f32[40,512]{1,0:T(8,128)S(1)} %get-tuple-element.193), channel_id=1, source_target_pairs={{0,16},{2,18},{4,20},{6,22},{8,24},{10,26},{12,28},{14,30},{16,0},... | collective-permute-start | bytes 245768 | tf_op jit(solution)/shard_map/ppermute | solution.py:647
  298.8 31.0 %collective-permute-start.32 = (f32[160,512]{1,0:T(8,128)S(1)}, f32[160,512]{1,0:T(8,128)S(1)}, u32[]{:S(2)}, u32[]{:S(2)}) collective-permute-start(f32[160,512]{1,0:T(8,128)S(1)} %pad_maximum_fusion.4), channel_id=1, source_target_pairs={{0,4},{2,6},{4,0},{6,2},{8,12},{10,14},{12,8},{14,10},{16,20},{18,... | collective-permute-start | bytes 983048 | tf_op jit(solution)/shard_map/ppermute | solution.py:647
  300.5 30.7 %collective-permute-start.37 = (f32[160,512]{1,0:T(8,128)S(1)}, f32[160,512]{1,0:T(8,128)S(1)}, u32[]{:S(2)}, u32[]{:S(2)}) collective-permute-start(f32[160,512]{1,0:T(8,128)S(1)} %pad_maximum_fusion.5), channel_id=1, source_target_pairs={{0,1},{1,0},{2,3},{3,2},{4,5},{5,4},{6,7},{7,6},{8,9},{9,8},{10,11... | collective-permute-start | bytes 983048 | tf_op jit(solution)/shard_map/ppermute | solution.py:647
  313.4 7.2 %collective-permute-start.26 = (f32[48,512]{1,0:T(8,128)S(1)}, f32[48,512]{1,0:T(8,128)S(1)}, u32[]{:S(2)}, u32[]{:S(2)}) collective-permute-start(f32[48,512]{1,0:T(8,128)S(1)} %pad_maximum_fusion.12), channel_id=1, source_target_pairs={{0,8},{2,10},{4,12},{6,14},{8,0},{10,2},{12,4},{14,6},{16,24},{18,... | collective-permute-start | bytes 294920 | tf_op jit(solution)/shard_map/ppermute | solution.py:647
  320.6 19.0 %collective-permute-start.27 = (f32[96,512]{1,0:T(8,128)S(1)}, f32[96,512]{1,0:T(8,128)S(1)}, u32[]{:S(2)}, u32[]{:S(2)}) collective-permute-start(f32[96,512]{1,0:T(8,128)S(1)} %pad_maximum_fusion.7), channel_id=1, source_target_pairs={{0,1},{1,0},{2,3},{3,2},{4,5},{5,4},{6,7},{7,6},{8,9},{9,8},{10,11... | collective-permute-start | bytes 589832 | tf_op jit(solution)/shard_map/ppermute | solution.py:647
  328.2 9.3 %collective-permute-start.19 = (f32[128,512]{1,0:T(8,128)S(1)}, f32[128,512]{1,0:T(8,128)S(1)}, u32[]{:S(2)}, u32[]{:S(2)}) collective-permute-start(f32[128,512]{1,0:T(8,128)S(1)} %pad_maximum_fusion.6), channel_id=1, source_target_pairs={{0,4},{2,6},{4,0},{6,2},{8,12},{10,14},{12,8},{14,10},{16,20},{18,... | collective-permute-start | bytes 786440 | tf_op jit(solution)/shard_map/ppermute | solution.py:647
  329.8 16.2 %collective-permute-start.33 = (f32[320,512]{1,0:T(8,128)S(1)}, f32[320,512]{1,0:T(8,128)S(1)}, u32[]{:S(2)}, u32[]{:S(2)}) collective-permute-start(f32[320,512]{1,0:T(8,128)S(1)} %pad_maximum_fusion), channel_id=1, source_target_pairs={{0,1},{1,0},{2,3},{3,2},{4,5},{5,4},{6,7},{7,6},{8,9},{9,8},{10,11... | collective-permute-start | bytes 1966088 | tf_op jit(solution)/shard_map/ppermute | solution.py:647
  331.3 21.2 %collective-permute-start.38 = (f32[320,512]{1,0:T(8,128)S(1)}, f32[320,512]{1,0:T(8,128)S(1)}, u32[]{:S(2)}, u32[]{:S(2)}) collective-permute-start(f32[320,512]{1,0:T(8,128)S(1)} %pad_maximum_fusion.1), channel_id=1, source_target_pairs={{0,4},{2,6},{4,0},{6,2},{8,12},{10,14},{12,8},{14,10},{16,20},{18,... | collective-permute-start | bytes 1966088 | tf_op jit(solution)/shard_map/ppermute | solution.py:647
  337.6 14.1 %collective-permute-start.20 = (f32[256,512]{1,0:T(8,128)S(1)}, f32[256,512]{1,0:T(8,128)S(1)}, u32[]{:S(2)}, u32[]{:S(2)}) collective-permute-start(f32[256,512]{1,0:T(8,128)S(1)} %pad_maximum_fusion.2), channel_id=1, source_target_pairs={{0,1},{1,0},{2,3},{3,2},{4,5},{5,4},{6,7},{7,6},{8,9},{9,8},{10,11... | collective-permute-start | bytes 1572872 | tf_op jit(solution)/shard_map/ppermute | solution.py:647
  339.7 14.1 %collective-permute-start.28 = (f32[192,512]{1,0:T(8,128)S(1)}, f32[192,512]{1,0:T(8,128)S(1)}, u32[]{:S(2)}, u32[]{:S(2)}) collective-permute-start(f32[192,512]{1,0:T(8,128)S(1)} %pad_maximum_fusion.3), channel_id=1, source_target_pairs={{0,4},{2,6},{4,0},{6,2},{8,12},{10,14},{12,8},{14,10},{16,20},{18,... | collective-permute-start | bytes 1179656 | tf_op jit(solution)/shard_map/ppermute | solution.py:647
  346.1 27.6 %collective-permute-start.34 = (f32[640,512]{1,0:T(8,128)S(1)}, f32[640,512]{1,0:T(8,128)}, u32[]{:S(2)}, u32[]{:S(2)}) collective-permute-start(f32[640,512]{1,0:T(8,128)S(1)} %constant_dynamic-update-slice_fusion.10.refs_0_), channel_id=1, source_target_pairs={{0,2},{2,0},{4,6},{6,4},{8,10},{10,8},{12,14},{14,12},{16,18},{18,... | collective-permute-start | bytes 3932168 | tf_op jit(solution)/shard_map/ppermute | solution.py:647
  352.5 17.0 %collective-permute-start.21 = (f32[512,512]{1,0:T(8,128)}, f32[512,512]{1,0:T(8,128)}, u32[]{:S(2)}, u32[]{:S(2)}) collective-permute-start(f32[512,512]{1,0:T(8,128)} %constant_dynamic-update-slice_fusion.refs_0_), channel_id=1, source_target_pairs={{0,2},{2,0},{4,6},{6,4},{8,10},{10,8},{12,14},{14,12},{16,18},{18,... | collective-permute-start | bytes 3145736 | tf_op jit(solution)/shard_map/ppermute | solution.py:647
  352.5 21.1 %collective-permute-start.39 = (f32[640,512]{1,0:T(8,128)S(1)}, f32[640,512]{1,0:T(8,128)}, u32[]{:S(2)}, u32[]{:S(2)}) collective-permute-start(f32[640,512]{1,0:T(8,128)S(1)} %constant_dynamic-update-slice_fusion.15.refs_2_), channel_id=1, source_target_pairs={{0,2},{2,0},{4,6},{6,4},{8,10},{10,8},{12,14},{14,12},{16,18},{18,... | collective-permute-start | bytes 3932168 | tf_op jit(solution)/shard_map/ppermute | solution.py:647
  354.6 14.9 %collective-permute-start.29 = (f32[384,512]{1,0:T(8,128)}, f32[384,512]{1,0:T(8,128)}, u32[]{:S(2)}, u32[]{:S(2)}) collective-permute-start(f32[384,512]{1,0:T(8,128)} %constant_dynamic-update-slice_fusion.5.refs_2_), channel_id=1, source_target_pairs={{0,2},{2,0},{4,6},{6,4},{8,10},{10,8},{12,14},{14,12},{16,18},{18,... | collective-permute-start | bytes 2359304 | tf_op jit(solution)/shard_map/ppermute | solution.py:647
  354.6 14.2 %all-to-all-start.3 = ((f32[32,8,128]{2,1,0:T(8,128)}), f32[32,8,128]{2,1,0:T(8,128)S(1)}, u32[]{:S(2)}, u32[]{:S(2)}) async-start(f32[32,8,128]{2,1,0:T(8,128)} %walk_backward.1), calls=%async_computation.3 | async-start | bytes 262144 | tf_op jit(solution)/shard_map/all_to_all | solution.py:910
  (56 other events, 318.3 us)
Sparse Core Ops, SparseCore 0:
  11.0 79.9 all-gather.2
